TPU v7x, 256 devices: a whole 4x4x8 slice. The times are simulated.
256 devices in a mesh: gx: 32 (over y, z_hi, x), vert: 8 (over z_lo, core).
Axes of the slice: x: 4, y: 4, z: 8 (z_hi: 2, z_lo: 4; z = z_hi * 4 + z_lo), core: 2. Of those that a mesh axis runs over, the one named last changes fastest.
Arguments:
- phase_field: float32 [128, 128, 32, 256], P('vert', 'gx'), may hold values from -0.2 to 1.2
- kappa_table: float32 [24, 3], replicated, may hold values from 0.2 to 2
- eps_table: float32 [12, 6], replicated, may hold values from -0.3 to 0.3
- orient_index: int32 [128], P('vert'), may hold values from 0 to 23
- family_index: int32 [128], P('vert'), may hold values from 0 to 11
Outputs:
- phase_next: float32 [128, 128, 32, 256], P('vert', 'gx')
- stress: float32 [6, 128, 32, 256], P(None, 'gx')
All inputs are finite; a program needn't handle non-finite values.
Results may differ from a plain program's by a relative error of at most 0.0003.
Values sent between devices are 32-bit elements; how exact they have to be, the bound alone decides.
No kernel may reach another device: no remote copies, remote signals or barrier semaphores. Data moves between devices by JAX's collectives and lax.ppermute only.
A program may use at most 64 MiB of HBM per device.

v0:
```python
import functools

import jax
import jax.numpy as jnp
import numpy as np
from jax import lax
from jax.experimental import pallas as pl
from jax.experimental.pallas import tpu as pltpu
from jax.sharding import PartitionSpec as P

LAME_LAMBDA = 1.5
SHEAR_MOD = 1.0
TIME_STEP = 0.1
CROSS_COUPLING = 0.02
TENSOR_SLOTS = ((0, 5, 4), (5, 1, 3), (4, 3, 2))
VOIGT_PAIRS = ((0, 0), (1, 1), (2, 2), (1, 2), (0, 2), (0, 1))
F32 = jnp.float32
BF16 = jnp.bfloat16
NX, NY, NZ = 128, 32, 256
SLAB = 4
SLABS = 32
HALF = NZ // 2
COMPS = 6


def z_table():
    z = np.arange(NZ)
    kz = np.arange(HALF)
    angle = 2 * np.pi * (np.outer(kz, z) % NZ) / NZ
    imag = -np.sin(angle)
    imag[0] = (-1.0) ** z
    return np.concatenate([np.cos(angle), imag])


def y_tables():
    general = np.zeros((2, SLAB, NY, 2, 2, SLAB, 16))
    packed = np.zeros((2, SLAB, NY, 2, 2, SLAB, 16))
    y = np.arange(NY)
    for half in range(2):
        for low in range(16):
            angle = 2 * np.pi * ((16 * half + low) * y % NY) / NY
            plain = 2 * np.pi * (low * y % NY) / NY
            for x in range(SLAB):
                general[0, x, :, half, 0, x, low] = np.cos(angle)
                general[1, x, :, half, 0, x, low] = np.sin(angle)
                general[0, x, :, half, 1, x, low] = -np.sin(angle)
                general[1, x, :, half, 1, x, low] = np.cos(angle)
                packed[half, x, :, half, 0, x, low] = np.cos(plain)
                packed[half, x, :, half, 1, x, low] = -np.sin(plain) if low else (-1.0) ** y
    return general.reshape(256, 256), packed.reshape(256, 256)


def x_tables():
    slab = np.arange(SLABS)
    angle = 2 * np.pi * (np.outer(slab, slab) % SLABS) / SLABS
    cosine, sine = np.cos(angle), np.sin(angle)
    left = np.zeros((COMPS, SLABS, 2, SLABS, 8))
    back = np.zeros((SLABS, 8, 2, COMPS, SLABS))
    for comp in range(COMPS):
        left[comp, :, 0, :, comp] = cosine
        left[comp, :, 1, :, comp] = sine
        back[:, comp, 0, comp, :] = cosine / NX
        back[:, comp, 1, comp, :] = -sine / NX
    lane = np.arange(128)
    plane = lane // 16 % SLAB
    turn = 2 * np.pi * np.outer(slab, plane) / NX
    right = np.zeros((2, SLAB, 16, 2, SLAB, 16))
    for plane_in in range(SLAB):
        for plane_out in range(SLAB):
            theta = 2 * np.pi * (plane_in * plane_out % SLAB) / SLAB
            for low in range(16):
                right[0, plane_in, low, 0, plane_out, low] = np.round(np.cos(theta))
                right[1, plane_in, low, 0, plane_out, low] = np.round(np.sin(theta))
                right[0, plane_in, low, 1, plane_out, low] = -np.round(np.sin(theta))
                right[1, plane_in, low, 1, plane_out, low] = np.round(np.cos(theta))
    right = right.reshape(128, 128)
    return left.reshape(192, 512), back.reshape(256, 384), np.cos(turn), np.sin(turn), right, right.T.copy()


def halves_of(table):
    full = np.asarray(table, np.float32)
    high = full.astype(jnp.bfloat16)
    low = (table - high.astype(np.float64)).astype(jnp.bfloat16)
    return jnp.asarray(high), jnp.asarray(low)


PLAIN = (((1,), (0,)), ((), ()))
RIGHT_T = (((1,), (1,)), ((), ()))
LEFT_T = (((0,), (0,)), ((), ()))


def split(value):
    high = value.astype(BF16)
    return high, (value - high.astype(F32)).astype(BF16)


def mul(a, b, dims):
    return lax.dot_general(a, b, dims, preferred_element_type=F32)


def dot3(left, right, dims=PLAIN):
    return mul(left[0], right[0], dims) + (mul(left[0], right[1], dims) + mul(left[1], right[0], dims))


def sums_kernel(core_ref, family_ref, eps_ref, phase_ref, tzh, tzl, ryh, ryl, rph, rpl, keep_ref, send_ref, eigen, square):
    step = pl.program_id(0)
    variants = phase_ref.shape[0]
    weight = [[eps_ref[family_ref[v], k] for k in range(COMPS)] for v in range(variants)]
    for tile in range(NY // 8):
        total = [None] * COMPS
        plain = None
        for v in range(variants):
            value = phase_ref[v, 0, tile * 8 : tile * 8 + 8, :]
            value = value * value
            plain = value if plain is None else plain + value
            for k in range(COMPS):
                term = weight[v][k] * value
                total[k] = term if total[k] is None else total[k] + term
        row = pl.multiple_of(step * NY + tile * 8, 8)
        square[pl.ds(row, 8), :] = plain
        for k in range(COMPS):
            eigen[pl.ds(k * 128 + row, 8), :] = total[k]

    @pl.when(step == SLAB - 1)
    def _():
        first = core_ref[0] == 0
        along_z = dot3((tzh[...], tzl[...]), split(eigen[...]), RIGHT_T)
        lines = []
        for k in range(COMPS):
            block = along_z[:, k * 128 : k * 128 + 128]
            lines.append(jnp.concatenate([block[:HALF], block[HALF:]], axis=1))
        packed_rows = jnp.concatenate([line[:8] for line in lines], axis=0)
        along_y = dot3(split(jnp.concatenate(lines, axis=0)), (ryh[...], ryl[...]))
        packed = dot3(split(packed_rows), (rph[...], rpl[...]))
        top = lax.broadcasted_iota(jnp.int32, (8, 256), 0) == 0
        for k in range(COMPS):
            block = along_y[k * 128 : k * 128 + 128]
            head = jnp.where(top, packed[k * 8 : k * 8 + 8], block[:8])
            block = jnp.concatenate([head, block[8:]], axis=0)
            keep_ref[pl.ds(k, 128, stride=8), :] = jnp.where(first, block[:, :128], block[:, 128:])
            send_ref[pl.ds(k, 128, stride=8), :] = jnp.where(first, block[:, 128:], block[:, :128])
        sums = square[...]
        keep_ref[pl.ds(6, 128, stride=8), :] = jnp.where(first, sums[:, :128], sums[:, 128:])
        send_ref[pl.ds(6, 128, stride=8), :] = jnp.where(first, sums[:, 128:], sums[:, :128])
        empty = jnp.zeros((128, 128), F32)
        keep_ref[pl.ds(7, 128, stride=8), :] = empty
        send_ref[pl.ds(7, 128, stride=8), :] = empty


def green_stress(strain, normals):
    trace_strain = strain[0] + strain[1] + strain[2]
    stiffened = [
        LAME_LAMBDA * trace_strain + 2.0 * SHEAR_MOD * strain[number] if number < 3 else 2.0 * SHEAR_MOD * strain[number]
        for number in range(6)
    ]
    traction = [sum(stiffened[TENSOR_SLOTS[row][col]] * normals[col] for col in range(3)) for row in range(3)]
    normal_part = normals[0] * traction[0] + normals[1] * traction[1] + normals[2] * traction[2]
    coupling = (LAME_LAMBDA + SHEAR_MOD) / (LAME_LAMBDA + 2.0 * SHEAR_MOD)
    shifted = [(traction[row] - normals[row] * normal_part * coupling) * (1.0 / SHEAR_MOD) for row in range(3)]
    excess = [
        0.5 * (normals[a] * shifted[b] + normals[b] * shifted[a]) - strain[number]
        for number, (a, b) in enumerate(VOIGT_PAIRS)
    ]
    trace_excess = excess[0] + excess[1] + excess[2]
    return [
        LAME_LAMBDA * trace_excess + 2.0 * SHEAR_MOD * excess[number] if number < 3 else 2.0 * SHEAR_MOD * excess[number]
        for number in range(6)
    ]


def unit(wave):
    length_sq = wave[0] * wave[0] + wave[1] * wave[1] + wave[2] * wave[2]
    positive = length_sq > 0
    inverse = jnp.where(positive, lax.rsqrt(jnp.where(positive, length_sq, 1.0)), 0.0)
    return [part * inverse for part in wave]


def spectral_kernel(place_ref, in_ref, lh, ll, bh, bl, tc_ref, ts_ref, right_ref, inverse_ref, out_ref):
    half, kz = place_ref[0], place_ref[1]
    rows = ((in_ref[:, 0] + in_ref[:, 1]) + (in_ref[:, 2] + in_ref[:, 3])).reshape(256, 128)
    lane1 = lax.broadcasted_iota(jnp.int32, (1, 128), 1)
    sign = jnp.where(lane1 < 64, 1.0, -1.0).astype(F32)

    def turned(value):
        return pltpu.roll(value, 64, 1) * sign

    flipped = rows * sign
    stacked = jnp.concatenate(
        [
            jnp.concatenate([rows, flipped], axis=1),
            jnp.concatenate([turned(rows), turned(flipped)], axis=1),
        ],
        axis=0,
    )
    spread = dot3((lh[...], ll[...]), split(stacked))
    both = jnp.concatenate([spread[:, :128], spread[:, 128:]], axis=0)
    cosine = tc_ref[...][None]
    sine = ts_ref[...][None]
    both = (both.reshape(12, 32, 128) * cosine + turned(both).reshape(12, 32, 128) * sine).reshape(384, 128)
    high, low = split(both)
    right = right_ref[...]
    hat = (mul(high, right, PLAIN) + mul(low, right, PLAIN)).reshape(12, 32, 128)

    row = lax.broadcasted_iota(jnp.int32, (32, 128), 0)
    lane = lax.broadcasted_iota(jnp.int32, (32, 128), 1)
    low_y = lane % 16
    kx = row + 32 * (lane // 16 % SLAB)
    plane = kz == 0
    ky = jnp.where(plane, low_y, 16 * half + low_y)
    wave_x = jnp.where(kx >= NX // 2, kx - NX, kx).astype(F32) * (1.0 / NX)
    wave_y = jnp.where(ky >= NY // 2, ky - NY, ky).astype(F32) * (1.0 / NY)
    kz_own = jnp.where(plane, jnp.where(half == 1, -HALF, 0), kz)
    wave_z = jnp.full((32, 128), kz_own, jnp.int32).astype(F32) * (1.0 / NZ)
    flip_x = jnp.where(kx == NX // 2, -wave_x, wave_x)
    flip_y = jnp.where(ky == NY // 2, -wave_y, wave_y)
    flip_z = jnp.where(jnp.full((32, 128), kz_own, jnp.int32) == -HALF, -wave_z, wave_z)
    special = jnp.logical_and(jnp.full((32, 128), kz, jnp.int32) == 0, low_y == 0)
    edge_y = jnp.full((32, 128), -0.5, F32)

    first, second = [], []
    for k in range(COMPS):
        a, b = hat[k], hat[k + COMPS]
        first.append(jnp.where(special, 0.5 * (a + b), a))
        second.append(jnp.where(special, 0.5 * (a - b), 0.0))
    parts = [
        green_stress(first, unit([wave_x, wave_y, wave_z])),
        green_stress(first, unit([flip_x, flip_y, flip_z])),
        green_stress(second, unit([wave_x, edge_y, wave_z])),
        green_stress(second, unit([flip_x, -edge_y, flip_z])),
    ]
    result = [0.5 * ((parts[0][k] + parts[1][k]) + (parts[2][k] + parts[3][k])) for k in range(COMPS)]

    high, low = split(jnp.concatenate(result, axis=0))
    inverse = inverse_ref[...]
    value = mul(high, inverse, PLAIN) + mul(low, inverse, PLAIN)
    value = (value.reshape(6, 32, 128) * cosine - turned(value).reshape(6, 32, 128) * sine).reshape(192, 128)
    stacked = jnp.concatenate([value, turned(value)], axis=0)
    answer = dot3((bh[...], bl[...]), split(stacked))
    kind = lax.broadcasted_iota(jnp.int32, (256, 128), 0) % 8
    answer = jnp.where(kind == 6, rows, answer).reshape(32, 8, 128)
    for copy in range(out_ref.shape[1]):
        out_ref[:, copy] = answer


def update_kernel(
    core_ref, family_ref, orient_ref, eps_ref, kappa_ref, mine_ref, other_ref, phase_ref, low_ref, high_ref,
    ryh, ryl, rph, rpl, tzh, tzl, next_ref, stress_ref, base,
):
    step = pl.program_id(0)

    @pl.when(step == 0)
    def _():
        first = core_ref[0] == 0

        def line(k):
            mine = mine_ref[pl.ds(k, 128, stride=8), :]
            other = other_ref[pl.ds(k, 128, stride=8), :]
            return jnp.concatenate([jnp.where(first, mine, other), jnp.where(first, other, mine)], axis=1)

        lines = [line(k) for k in range(COMPS)]
        packed = dot3(split(jnp.concatenate([block[:8] for block in lines], axis=0)), (rph[...], rpl[...]))
        along_y = dot3(split(jnp.concatenate(lines, axis=0)), (ryh[...], ryl[...]))
        top = lax.broadcasted_iota(jnp.int32, (8, 256), 0) == 0
        for k in range(COMPS):
            block = along_y[k * 128 : k * 128 + 128]
            head = jnp.where(top, packed[k * 8 : k * 8 + 8], block[:8])
            block = jnp.concatenate([head, block[8:]], axis=0)
            block = jnp.concatenate([block[:, :128], block[:, 128:]], axis=0)
            cells = dot3(split(block.T), (tzh[...], tzl[...]))
            stress_ref[k] = cells.reshape(SLAB, NY, NZ)
        base[...] = (2.0 + 2.0 * CROSS_COUPLING * line(6)).reshape(SLAB, NY, NZ)

    per_step = phase_ref.shape[0]
    for index in range(per_step):
        variant = step * per_step + index
        family = family_ref[variant]
        orient = orient_ref[variant]
        weight = [eps_ref[family, k] * (-2.0 if k < 3 else -4.0) for k in range(COMPS)]
        kappa = [TIME_STEP * kappa_ref[orient, d] for d in range(3)]
        center = 1.0 - 2.0 * (0.0 + kappa[0] + kappa[1] + kappa[2])
        for x in range(SLAB):
            p = phase_ref[index, x]
            before = low_ref[index, 0] if x == 0 else phase_ref[index, x - 1]
            after = high_ref[index, 0] if x == SLAB - 1 else phase_ref[index, x + 1]
            slope = base[x]
            for k in range(COMPS):
                slope = slope + weight[k] * stress_ref[k, x]
            slope = slope + p * (-6.0 + (4.0 - 2.0 * CROSS_COUPLING) * p)
            moved = kappa[0] * (before + after)
            moved = moved + kappa[1] * (pltpu.roll(p, 1, 0) + pltpu.roll(p, NY - 1, 0))
            moved = moved + kappa[2] * (pltpu.roll(p, 1, 1) + pltpu.roll(p, NZ - 1, 1))
            next_ref[index, x] = p * (center - TIME_STEP * slope) + moved


def vmem():
    return pl.BlockSpec(memory_space=pltpu.VMEM)


def smem():
    return pl.BlockSpec(memory_space=pltpu.SMEM)


def ring(count, shift):
    return [(i, (i + shift) % count) for i in range(count)]


def body(phase_field, kappa_table, eps_table, orient_index, family_index):
    slabs = lax.axis_size("gx")
    groups = lax.axis_size("vert")
    runs = groups // 2
    variants = phase_field.shape[0]
    place = lax.axis_index("vert")
    core = (place % 2).astype(jnp.int32)
    kz_own = (lax.axis_index("gx") * runs + place // 2).astype(jnp.int32)
    core_arr = core.reshape(1)
    place_arr = jnp.stack([core, kz_own])

    low_plane = lax.ppermute(lax.slice_in_dim(phase_field, SLAB - 1, SLAB, axis=1), "gx", ring(slabs, 1))
    high_plane = lax.ppermute(lax.slice_in_dim(phase_field, 0, 1, axis=1), "gx", ring(slabs, -1))

    tz = z_table()
    ry, rp = y_tables()
    left, back, tc, ts, right, right_t = x_tables()

    spread = jax.ShapeDtypeStruct((1024, 128), F32)
    keep, send = pl.pallas_call(
        sums_kernel,
        grid=(SLAB,),
        in_specs=[smem(), smem(), smem(), pl.BlockSpec((variants, 1, NY, NZ), lambda i: (0, i, 0, 0))] + [vmem()] * 6,
        out_specs=[pl.BlockSpec((1024, 128), lambda i: (0, 0))] * 2,
        out_shape=[spread, spread],
        scratch_shapes=[pltpu.VMEM((COMPS * 128, NZ), F32), pltpu.VMEM((128, NZ), F32)],
        name="sums",
    )(core_arr, family_index, eps_table, phase_field, *halves_of(tz), *halves_of(ry), *halves_of(rp))

    partner = [(i, i ^ 1) for i in range(groups)]
    same_core = [[g * groups + 2 * r + c for g in range(slabs) for r in range(runs)] for c in range(2)]

    def exchange(value):
        return lax.all_to_all(
            value, ("gx", "vert"), split_axis=0, concat_axis=0, axis_index_groups=same_core, tiled=True
        )

    summed = keep + lax.ppermute(send, "vert", partner)
    arrived = exchange(summed.reshape(128, 8, 128)).reshape(slabs, runs, 8, 128)

    answers = pl.pallas_call(
        spectral_kernel,
        in_specs=[smem()] + [vmem()] * 9,
        out_specs=vmem(),
        out_shape=jax.ShapeDtypeStruct((slabs, runs, 8, 128), F32),
        name="spectral",
    )(
        place_arr, arrived, *halves_of(left), *halves_of(back), jnp.asarray(tc, F32), jnp.asarray(ts, F32),
        jnp.asarray(right, BF16), jnp.asarray(right_t, BF16),
    )

    mine = exchange(answers.reshape(128, 8, 128)).reshape(1024, 128)
    other = lax.ppermute(mine, "vert", partner)

    per_step = 2
    phase_next, stress = pl.pallas_call(
        update_kernel,
        grid=(variants // per_step,),
        in_specs=[smem()] * 5
        + [vmem()] * 2
        + [
            pl.BlockSpec((per_step, SLAB, NY, NZ), lambda i: (i, 0, 0, 0)),
            pl.BlockSpec((per_step, 1, NY, NZ), lambda i: (i, 0, 0, 0)),
            pl.BlockSpec((per_step, 1, NY, NZ), lambda i: (i, 0, 0, 0)),
        ]
        + [vmem()] * 6,
        out_specs=[
            pl.BlockSpec((per_step, SLAB, NY, NZ), lambda i: (i, 0, 0, 0)),
            pl.BlockSpec((COMPS, SLAB, NY, NZ), lambda i: (0, 0, 0, 0)),
        ],
        out_shape=[
            jax.ShapeDtypeStruct(phase_field.shape, F32),
            jax.ShapeDtypeStruct((COMPS, SLAB, NY, NZ), F32),
        ],
        scratch_shapes=[pltpu.VMEM((SLAB, NY, NZ), F32)],
        name="update",
    )(
        core_arr, family_index, orient_index, eps_table, kappa_table, mine, other, phase_field, low_plane, high_plane,
        *halves_of(np.linalg.inv(ry)), *halves_of(np.linalg.inv(rp)), *halves_of(np.linalg.inv(tz).T),
    )
    return phase_next, stress


def solution(mesh):
    return jax.shard_map(
        body,
        mesh=mesh,
        in_specs=(P("vert", "gx", None, None), P(), P(), P("vert"), P("vert")),
        out_specs=(P("vert", "gx", None, None), P(None, "gx", None, None)),
        check_vma=False,
    )
```

profile of v0, /device:TPU:32, one launch (start us, length us, event | category | flops | bytes accessed | tf_op | source)
XLA Modules:
  0.0 110.8 jit_solution(1615457966098960932)
XLA Ops:
  0.6 1.4 %copy.28.eps_ref = f32[12,6]{1,0:T(8,128)} copy(f32[12,6]{0,1:T(8,128)} %param.27) | data formatting | bytes 576 | tf_op args[2]
  2.0 5.5 %sums.1 = (f32[1024,128]{1,0:T(8,128)}, f32[1024,128]{1,0:T(8,128)}) custom-call(s32[1]{0:T(128)} %bitcast.core_ref, s32[16]{0:T(128)} %family_ref.3, f32[12,6]{1,0:T(8,128)} %copy.28.eps_ref, f32[16,4,32,256]{3,2,1,0:T(8,128)} %phase_ref.3, bf16[256,256]{1,0:T(8,128)(2,1)} %constant.75.clone.tzh, bf16[256,256]{1,0:T(8,128)(2,1)} %constant.76.clone.tzl, ...), custom_call_target="tpu_custom_call" | custom-call | tf_op jit(solution)/shard_map/sums/pallas_call | solution.py:326
  7.5 0.0 collective-permute-start
  7.5 2.1 %collective-permute-done = f32[1024,128]{1,0:T(8,128)S(1)} collective-permute-done((f32[1024,128]{1,0:T(8,128)}, f32[1024,128]{1,0:T(8,128)S(1)}, u32[]{:S(2)}, u32[]{:S(2)}) %collective-permute-start) | collective-permute-done | bytes 524320 | tf_op jit(solution)/shard_map/ppermute | solution.py:344
  9.6 1.9 %add_bitcast_fusion = f32[128,8,128]{2,1,0:T(8,128)} fusion(f32[1024,128]{1,0:T(8,128)} %get-tuple-element.4, f32[1024,128]{1,0:T(8,128)S(1)} %collective-permute-done), kind=kLoop, calls=%fused_computation | loop fusion | flops 131072 | bytes 1572864 | tf_op jit(solution)/shard_map/reshape | solution.py:345
  11.5 0.0 copy-start
  11.5 15.1 %all-to-all-start = ((f32[128,8,128]{2,1,0:T(8,128)}), f32[128,8,128]{2,1,0:T(8,128)S(1)}, u32[]{:S(2)}, u32[]{:S(2)}) async-start(f32[128,8,128]{2,1,0:T(8,128)} %add_bitcast_fusion), calls=%async_computation | async-start | bytes 1048576 | tf_op jit(solution)/shard_map/all_to_all | solution.py:340
  26.7 0.6 pad_add_fusion.place_ref
  27.3 19.8 %all-to-all-done = f32[128,8,128]{2,1,0:T(8,128)S(1)} async-done(((f32[128,8,128]{2,1,0:T(8,128)}), f32[128,8,128]{2,1,0:T(8,128)S(1)}, u32[]{:S(2)}, u32[]{:S(2)}) %all-to-all-start) | async-done | bytes 524320 | tf_op jit(solution)/shard_map/all_to_all | solution.py:340
  47.1 0.0 copy-start.2
  47.1 0.8 copy-done.2
  47.9 0.0 copy-start.6
  47.9 3.8 %spectral.1 = f32[32,4,8,128]{3,2,1,0:T(8,128)} custom-call(s32[2]{0:T(128)} %pad_add_fusion.place_ref, f32[32,4,8,128]{3,2,1,0:T(8,128)} %bitcast.9, bf16[192,512]{1,0:T(8,128)(2,1)} %constant.81.clone.lh, bf16[192,512]{1,0:T(8,128)(2,1)} %constant.82.clone.ll, bf16[256,384]{1,0:T(8,128)(2,1)} %constant.83.clone.bh, bf16[256,384]{1,0:T(8,128)(2,1)} %constant.84.clone.bl, ...), custom_call_target="tpu_custom_call" | custom-call | tf_op jit(solution)/shard_map/spectral/pallas_call | solution.py:347
  51.7 6.6 %all-to-all-start.1 = ((f32[128,8,128]{2,1,0:T(8,128)}), f32[128,8,128]{2,1,0:T(8,128)S(1)}, u32[]{:S(2)}, u32[]{:S(2)}) async-start(f32[128,8,128]{2,1,0:T(8,128)} %bitcast.10), calls=%async_computation.1 | async-start | bytes 1048576 | tf_op jit(solution)/shard_map/all_to_all | solution.py:340
  58.3 0.0 copy-done
  58.3 0.9 fusion
  59.2 9.5 %collective-permute-start.3 = (f32[16,1,32,256]{3,2,1,0:T(8,128)}, f32[16,1,32,256]{3,2,1,0:T(8,128)S(1)}, u32[]{:S(2)}, u32[]{:S(2)}) collective-permute-start(f32[16,1,32,256]{3,2,1,0:T(8,128)} %get-tuple-element.6), channel_id=1, source_target_pairs={{0,248},{8,0},{16,8},{24,16},{32,24},{40,32},{48,40},{56,48},{64,5... | collective-permute-start | bytes 1572872 | tf_op jit(solution)/shard_map/ppermute | solution.py:319
  68.7 0.0 collective-permute-start.2
  68.7 9.4 %all-to-all-done.1 = f32[128,8,128]{2,1,0:T(8,128)S(1)} async-done(((f32[128,8,128]{2,1,0:T(8,128)}), f32[128,8,128]{2,1,0:T(8,128)S(1)}, u32[]{:S(2)}, u32[]{:S(2)}) %all-to-all-start.1) | async-done | bytes 524320 | tf_op jit(solution)/shard_map/all_to_all | solution.py:340
  78.1 0.0 copy-start.1
  78.1 0.0 collective-permute-start.1
  78.1 0.0 copy-done.6
  78.1 0.8 copy.29.kappa_ref
  78.9 11.3 %collective-permute-done.3.high_ref = f32[16,1,32,256]{3,2,1,0:T(8,128)S(1)} collective-permute-done((f32[16,1,32,256]{3,2,1,0:T(8,128)}, f32[16,1,32,256]{3,2,1,0:T(8,128)S(1)}, u32[]{:S(2)}, u32[]{:S(2)}) %collective-permute-start.3) | collective-permute-done | bytes 524320 | tf_op jit(solution)/shard_map/ppermute | solution.py:319
  90.2 0.0 copy-start.3
  90.2 9.8 %collective-permute-done.2.low_ref = f32[16,1,32,256]{3,2,1,0:T(8,128)S(1)} collective-permute-done((f32[16,1,32,256]{3,2,1,0:T(8,128)S(1)}, f32[16,1,32,256]{3,2,1,0:T(8,128)S(1)}, u32[]{:S(2)}, u32[]{:S(2)}) %collective-permute-start.2) | collective-permute-done | bytes 524320 | tf_op jit(solution)/shard_map/ppermute | solution.py:318
  100.0 0.0 copy-start.4
  100.0 0.0 collective-permute-done.1.other_ref
  100.0 0.0 copy-done.1
  100.0 0.0 copy-done.3
  100.1 0.8 copy-done.4
  100.9 0.0 copy-start.5
  100.9 0.8 copy-done.5
  101.7 9.1 %update.1 = (f32[16,4,32,256]{3,2,1,0:T(8,128)}, f32[6,4,32,256]{3,2,1,0:T(8,128)}) custom-call(s32[1]{0:T(128)} %bitcast.core_ref, s32[16]{0:T(128)} %family_ref.3, s32[16]{0:T(128)} %orient_ref.1, f32[12,6]{1,0:T(8,128)} %copy.28.eps_ref, f32[24,3]{1,0:T(8,128)} %copy.29.kappa_ref, f32[1024,128]{1,0:T(8,128)} %bitcast.8, f32[1024,128]{1,0:T(8,128)} %copy-done.5, ...), custom_call_target="tpu_custom_call" | custom-call | tf_op jit(solution)/shard_map/update/pallas_call | solution.py:362
Async XLA Ops:
  7.5 2.1 %collective-permute-start = (f32[1024,128]{1,0:T(8,128)}, f32[1024,128]{1,0:T(8,128)S(1)}, u32[]{:S(2)}, u32[]{:S(2)}) collective-permute-start(f32[1024,128]{1,0:T(8,128)} %get-tuple-element.5), channel_id=1, source_target_pairs={{0,1},{1,0},{2,3},{3,2},{4,5},{5,4},{6,7},{7,6},{8,9},{9,8},{10,11... | collective-permute-start | bytes 1572872 | tf_op jit(solution)/shard_map/ppermute | solution.py:344
  11.5 46.7 %copy-start = (f32[16,4,32,256]{3,2,1,0:T(8,128)S(1)}, f32[16,4,32,256]{3,2,1,0:T(8,128)}, u32[]{:S(2)}) copy-start(f32[16,4,32,256]{3,2,1,0:T(8,128)} %phase_ref.3) | copy-start | bytes 6291460
  11.5 35.6 %all-to-all-start = ((f32[128,8,128]{2,1,0:T(8,128)}), f32[128,8,128]{2,1,0:T(8,128)S(1)}, u32[]{:S(2)}, u32[]{:S(2)}) async-start(f32[128,8,128]{2,1,0:T(8,128)} %add_bitcast_fusion), calls=%async_computation | async-start | bytes 1048576 | tf_op jit(solution)/shard_map/all_to_all | solution.py:340
  47.1 0.8 copy-start.2
  47.9 30.2 %copy-start.6 = (f32[24,3]{0,1:T(4,128)S(1)}, f32[24,3]{0,1:T(4,128)}, u32[]{:S(2)}) copy-start(f32[24,3]{0,1:T(4,128)} %param.26) | copy-start | bytes 868
  51.7 26.4 %all-to-all-start.1 = ((f32[128,8,128]{2,1,0:T(8,128)}), f32[128,8,128]{2,1,0:T(8,128)S(1)}, u32[]{:S(2)}, u32[]{:S(2)}) async-start(f32[128,8,128]{2,1,0:T(8,128)} %bitcast.10), calls=%async_computation.1 | async-start | bytes 1048576 | tf_op jit(solution)/shard_map/all_to_all | solution.py:340
  59.2 31.1 %collective-permute-start.3 = (f32[16,1,32,256]{3,2,1,0:T(8,128)}, f32[16,1,32,256]{3,2,1,0:T(8,128)S(1)}, u32[]{:S(2)}, u32[]{:S(2)}) collective-permute-start(f32[16,1,32,256]{3,2,1,0:T(8,128)} %get-tuple-element.6), channel_id=1, source_target_pairs={{0,248},{8,0},{16,8},{24,16},{32,24},{40,32},{48,40},{56,48},{64,5... | collective-permute-start | bytes 1572872 | tf_op jit(solution)/shard_map/ppermute | solution.py:319
  68.7 31.3 %collective-permute-start.2 = (f32[16,1,32,256]{3,2,1,0:T(8,128)S(1)}, f32[16,1,32,256]{3,2,1,0:T(8,128)S(1)}, u32[]{:S(2)}, u32[]{:S(2)}) collective-permute-start(f32[16,1,32,256]{3,2,1,0:T(8,128)S(1)} %get-tuple-element.7), channel_id=1, source_target_pairs={{0,8},{8,16},{16,24},{24,32},{32,40},{40,48},{48,56},{56,64},{64,7... | collective-permute-start | bytes 1572872 | tf_op jit(solution)/shard_map/ppermute | solution.py:318
  78.1 21.9 %copy-start.1 = (f32[128,8,128]{2,1,0:T(8,128)}, f32[128,8,128]{2,1,0:T(8,128)S(1)}, u32[]{:S(2)}) copy-start(f32[128,8,128]{2,1,0:T(8,128)S(1)} %all-to-all-done.1) | copy-start | bytes 1572868
  78.1 21.9 %collective-permute-start.1 = (f32[1024,128]{1,0:T(8,128)S(1)}, f32[1024,128]{1,0:T(8,128)S(1)}, u32[]{:S(2)}, u32[]{:S(2)}) collective-permute-start(f32[1024,128]{1,0:T(8,128)S(1)} %bitcast.7), channel_id=1, source_target_pairs={{0,1},{1,0},{2,3},{3,2},{4,5},{5,4},{6,7},{7,6},{8,9},{9,8},{10,11... | collective-permute-start | bytes 1572872 | tf_op jit(solution)/shard_map/ppermute | solution.py:359
  90.2 9.8 %copy-start.3 = (f32[16,1,32,256]{3,2,1,0:T(8,128)}, f32[16,1,32,256]{3,2,1,0:T(8,128)S(1)}, u32[]{:S(2)}) copy-start(f32[16,1,32,256]{3,2,1,0:T(8,128)S(1)} %collective-permute-done.3.high_ref) | copy-start | bytes 1572868
  100.0 0.8 copy-start.4
  100.9 0.8 copy-start.5
where the time goes:
time: 111 us
  waiting for transfers between devices  52.5 us (47%)
  starting transfers between devices  31.2 us (28%)
  Pallas kernels  18.4 us (17%)
  local copies, waits for them, and re-layouts  5.45 us (5%)
  other arithmetic  2.52 us (2%)
    all_to_all x2, waiting for transfers between devices, exchange(): lax.all_to_all(value, ('gx', 'vert'), split_axis=0, concat_axis=0, axis_i...  29.2 us
    all_to_all x2, starting transfers between devices, exchange(): lax.all_to_all(value, ('gx', 'vert'), split_axis=0, concat_axis=0, axis_i...  21.7 us
    ppermute x1, waiting for transfers between devices, body(): lax.ppermute(lax.slice_in_dim(phase_field, 0, 1, axis=1), 'gx', ring(slab...  11.3 us
    ppermute x1, waiting for transfers between devices, body(): lax.ppermute(lax.slice_in_dim(phase_field, SLAB - 1, SLAB, axis=1), 'gx',...  9.79 us
    ppermute x1, starting transfers between devices, body(): lax.ppermute(lax.slice_in_dim(phase_field, 0, 1, axis=1), 'gx', ring(slab...  9.54 us
    pallas_call x1, Pallas kernels, body(): pl.pallas_call(update_kernel, grid=(variants // per_step,), in_specs=[sme...  9.11 us
    pallas_call x1, Pallas kernels, body(): pl.pallas_call(sums_kernel, grid=(SLAB,), in_specs=[smem(), smem(), smem(...  5.49 us
    unnamed x16, local copies, waits for them, and re-layouts  4.56 us
  transfers between devices with their start and end apart: 6, of which 5 were waited for; matrix products, arithmetic and copies ran while one was open for 2% of the time, Pallas kernels for 0%

commit v1 on v0

v1 whole, which is shorter than its diff:
```python
import jax
import jax.numpy as jnp
import numpy as np
from jax import lax
from jax.experimental import pallas as pl
from jax.experimental.pallas import tpu as pltpu
from jax.sharding import PartitionSpec as P


LAME_LAMBDA = 1.5
SHEAR_MOD = 1.0
TIME_STEP = 0.1
CROSS_COUPLING = 0.02
TENSOR_SLOTS = ((0, 5, 4), (5, 1, 3), (4, 3, 2))
VOIGT_PAIRS = ((0, 0), (1, 1), (2, 2), (1, 2), (0, 2), (0, 1))
F32 = jnp.float32
BF16 = jnp.bfloat16
NX, NY, NZ = 128, 32, 256
SLAB = 4
SLABS = 32
HALF = NZ // 2
COMPS = 6


def z_table():
    z = np.arange(NZ)
    kz = np.arange(HALF)
    angle = 2 * np.pi * (np.outer(kz, z) % NZ) / NZ
    imag = -np.sin(angle)
    imag[0] = (-1.0) ** z
    return np.concatenate([np.cos(angle), imag])


def y_tables():
    general = np.zeros((2, SLAB, NY, 2, 2, SLAB, 16))
    packed = np.zeros((2, SLAB, NY, 2, 2, SLAB, 16))
    y = np.arange(NY)
    for half in range(2):
        for low in range(16):
            angle = 2 * np.pi * ((16 * half + low) * y % NY) / NY
            plain = 2 * np.pi * (low * y % NY) / NY
            for x in range(SLAB):
                general[0, x, :, half, 0, x, low] = np.cos(angle)
                general[1, x, :, half, 0, x, low] = np.sin(angle)
                general[0, x, :, half, 1, x, low] = -np.sin(angle)
                general[1, x, :, half, 1, x, low] = np.cos(angle)
                packed[half, x, :, half, 0, x, low] = np.cos(plain)
                packed[half, x, :, half, 1, x, low] = -np.sin(plain) if low else (-1.0) ** y
    return general.reshape(256, 256), packed.reshape(256, 256)


def x_tables():
    slab = np.arange(SLABS)
    angle = 2 * np.pi * (np.outer(slab, slab) % SLABS) / SLABS
    cosine, sine = np.cos(angle), np.sin(angle)
    left = np.zeros((COMPS, SLABS, 2, SLABS, 8))
    back = np.zeros((SLABS, 8, 2, COMPS, SLABS))
    for comp in range(COMPS):
        left[comp, :, 0, :, comp] = cosine
        left[comp, :, 1, :, comp] = sine
        back[:, comp, 0, comp, :] = cosine / NX
        back[:, comp, 1, comp, :] = -sine / NX
    lane = np.arange(128)
    plane = lane // 16 % SLAB
    turn = 2 * np.pi * np.outer(slab, plane) / NX
    right = np.zeros((2, SLAB, 16, 2, SLAB, 16))
    for plane_in in range(SLAB):
        for plane_out in range(SLAB):
            theta = 2 * np.pi * (plane_in * plane_out % SLAB) / SLAB
            for low in range(16):
                right[0, plane_in, low, 0, plane_out, low] = np.round(np.cos(theta))
                right[1, plane_in, low, 0, plane_out, low] = np.round(np.sin(theta))
                right[0, plane_in, low, 1, plane_out, low] = -np.round(np.sin(theta))
                right[1, plane_in, low, 1, plane_out, low] = np.round(np.cos(theta))
    right = right.reshape(128, 128)
    return left.reshape(192, 512), back.reshape(256, 384), np.cos(turn), np.sin(turn), right, right.T.copy()


def halves_of(table):
    full = np.asarray(table, np.float32)
    high = full.astype(jnp.bfloat16)
    low = (table - high.astype(np.float64)).astype(jnp.bfloat16)
    return high, low


def stacked_halves(*tables):
    parts = [half for table in tables for half in halves_of(table)]
    return jnp.asarray(np.stack(parts))


def spectral_tables(left, back, tc, ts, right, right_t):
    packed = np.zeros((896, 512), jnp.bfloat16)
    left_high, left_low = halves_of(left)
    back_high, back_low = halves_of(back)
    packed[0:192], packed[192:384] = left_high, left_low
    packed[384:640, :384], packed[640:896, :384] = back_high, back_low
    packed[384:512, 384:], packed[512:640, 384:] = right, right_t
    for index, part in enumerate(halves_of(tc) + halves_of(ts)):
        packed[640 + 32 * index : 672 + 32 * index, 384:] = part
    return jnp.asarray(packed)


PLAIN = (((1,), (0,)), ((), ()))
RIGHT_T = (((1,), (1,)), ((), ()))


def split(value):
    high = value.astype(BF16)
    return high, (value - high.astype(F32)).astype(BF16)


def mul(a, b, dims):
    return lax.dot_general(a, b, dims, preferred_element_type=F32)


def dot3(left, right, dims=PLAIN):
    return mul(left[0], right[0], dims) + (mul(left[0], right[1], dims) + mul(left[1], right[0], dims))


def sums_kernel(
    place_ref, family_ref, eps_ref, phase_hbm, table_hbm,
    keep_ref, send_ref, last_a, last_b, front_a, front_b, phase, table, eigen, square, sems,
):
    variants = phase.shape[0]
    loads = [pltpu.make_async_copy(phase_hbm.at[:, x], phase.at[:, x], sems.at[x]) for x in range(SLAB)]
    loads.append(pltpu.make_async_copy(table_hbm, table, sems.at[SLAB]))
    for load in loads:
        load.start()
    weight = [[eps_ref[k, family_ref[v]] for k in range(COMPS)] for v in range(variants)]
    for x in range(SLAB):
        loads[x].wait()

        def tile_sum(tile, carry, x=x):
            row = pl.multiple_of(tile * 8, 8)
            total = [None] * COMPS
            plain = None
            for v in range(variants):
                value = phase[v, x, pl.ds(row, 8), :]
                value = value * value
                plain = value if plain is None else plain + value
                for k in range(COMPS):
                    term = weight[v][k] * value
                    total[k] = term if total[k] is None else total[k] + term
            square[pl.ds(x * NY + row, 8), :] = plain
            for k in range(COMPS):
                eigen[pl.ds(k * 128 + x * NY + row, 8), :] = total[k]
            return carry

        lax.fori_loop(0, NY // 8, tile_sum, 0)
        if x in (0, SLAB - 1):
            low_half, high_half = (front_a, front_b) if x == 0 else (last_a, last_b)
            low_half[...] = phase[: variants // 2, x]
            high_half[...] = phase[variants // 2 :, x]
    loads[SLAB].wait()

    first = place_ref[0] == 0
    along_z = dot3((table[0], table[1]), split(eigen[...]), RIGHT_T)
    lines = []
    for k in range(COMPS):
        block = along_z[:, k * 128 : k * 128 + 128]
        lines.append(jnp.concatenate([block[:HALF], block[HALF:]], axis=1))
    packed_rows = jnp.concatenate([line[:8] for line in lines], axis=0)
    along_y = dot3(split(jnp.concatenate(lines, axis=0)), (table[2], table[3]))
    packed = dot3(split(packed_rows), (table[4], table[5]))
    top = lax.broadcasted_iota(jnp.int32, (8, 256), 0) == 0
    for k in range(COMPS):
        block = along_y[k * 128 : k * 128 + 128]
        head = jnp.where(top, packed[k * 8 : k * 8 + 8], block[:8])
        block = jnp.concatenate([head, block[8:]], axis=0)
        keep_ref[pl.ds(k, 128, stride=8), :] = jnp.where(first, block[:, :128], block[:, 128:])
        send_ref[pl.ds(k, 128, stride=8), :] = jnp.where(first, block[:, 128:], block[:, :128])
    sums = square[...]
    keep_ref[pl.ds(6, 128, stride=8), :] = jnp.where(first, sums[:, :128], sums[:, 128:])
    send_ref[pl.ds(6, 128, stride=8), :] = jnp.where(first, sums[:, 128:], sums[:, :128])
    empty = jnp.zeros((128, 128), F32)
    keep_ref[pl.ds(7, 128, stride=8), :] = empty
    send_ref[pl.ds(7, 128, stride=8), :] = empty


def green_stress(strain, normals):
    trace_strain = strain[0] + strain[1] + strain[2]
    stiffened = [
        LAME_LAMBDA * trace_strain + 2.0 * SHEAR_MOD * strain[number] if number < 3 else 2.0 * SHEAR_MOD * strain[number]
        for number in range(6)
    ]
    traction = [sum(stiffened[TENSOR_SLOTS[row][col]] * normals[col] for col in range(3)) for row in range(3)]
    normal_part = normals[0] * traction[0] + normals[1] * traction[1] + normals[2] * traction[2]
    coupling = (LAME_LAMBDA + SHEAR_MOD) / (LAME_LAMBDA + 2.0 * SHEAR_MOD)
    shifted = [(traction[row] - normals[row] * normal_part * coupling) * (1.0 / SHEAR_MOD) for row in range(3)]
    excess = [
        0.5 * (normals[a] * shifted[b] + normals[b] * shifted[a]) - strain[number]
        for number, (a, b) in enumerate(VOIGT_PAIRS)
    ]
    trace_excess = excess[0] + excess[1] + excess[2]
    return [
        LAME_LAMBDA * trace_excess + 2.0 * SHEAR_MOD * excess[number] if number < 3 else 2.0 * SHEAR_MOD * excess[number]
        for number in range(6)
    ]


def unit(wave):
    length_sq = wave[0] * wave[0] + wave[1] * wave[1] + wave[2] * wave[2]
    positive = length_sq > 0
    inverse = jnp.where(positive, lax.rsqrt(jnp.where(positive, length_sq, 1.0)), 0.0)
    return [part * inverse for part in wave]


def spectral_kernel(place_ref, in_ref, table, out_ref):
    half, kz = place_ref[0], place_ref[1]
    rows = ((in_ref[:, 0] + in_ref[:, 1]) + (in_ref[:, 2] + in_ref[:, 3])).reshape(256, 128)
    lane1 = lax.broadcasted_iota(jnp.int32, (1, 128), 1)
    sign = jnp.where(lane1 < 64, 1.0, -1.0).astype(F32)

    def turned(value):
        return pltpu.roll(value, 64, 1) * sign

    flipped = rows * sign
    stacked = jnp.concatenate(
        [
            jnp.concatenate([rows, flipped], axis=1),
            jnp.concatenate([turned(rows), turned(flipped)], axis=1),
        ],
        axis=0,
    )
    spread = dot3((table[0:192], table[192:384]), split(stacked))
    both = jnp.concatenate([spread[:, :128], spread[:, 128:]], axis=0)
    turns = table[640:768, 384:].astype(F32)
    cosine = (turns[0:32] + turns[32:64])[None]
    sine = (turns[64:96] + turns[96:128])[None]
    both = (both.reshape(12, 32, 128) * cosine + turned(both).reshape(12, 32, 128) * sine).reshape(384, 128)
    high, low = split(both)
    right = table[384:512, 384:]
    hat = (mul(high, right, PLAIN) + mul(low, right, PLAIN)).reshape(12, 32, 128)

    row = lax.broadcasted_iota(jnp.int32, (32, 128), 0)
    lane = lax.broadcasted_iota(jnp.int32, (32, 128), 1)
    low_y = lane % 16
    kx = row + 32 * (lane // 16 % SLAB)
    plane = kz == 0
    ky = jnp.where(plane, low_y, 16 * half + low_y)
    wave_x = jnp.where(kx >= NX // 2, kx - NX, kx).astype(F32) * (1.0 / NX)
    wave_y = jnp.where(ky >= NY // 2, ky - NY, ky).astype(F32) * (1.0 / NY)
    kz_own = jnp.where(plane, jnp.where(half == 1, -HALF, 0), kz)
    wave_z = jnp.full((32, 128), kz_own, jnp.int32).astype(F32) * (1.0 / NZ)
    flip_x = jnp.where(kx == NX // 2, -wave_x, wave_x)
    flip_y = jnp.where(ky == NY // 2, -wave_y, wave_y)
    flip_z = jnp.where(jnp.full((32, 128), kz_own, jnp.int32) == -HALF, -wave_z, wave_z)
    special = jnp.logical_and(jnp.full((32, 128), kz, jnp.int32) == 0, low_y == 0)
    edge_y = jnp.full((32, 128), -0.5, F32)

    first, second = [], []
    for k in range(COMPS):
        a, b = hat[k], hat[k + COMPS]
        first.append(jnp.where(special, 0.5 * (a + b), a))
        second.append(jnp.where(special, 0.5 * (a - b), 0.0))
    parts = [
        green_stress(first, unit([wave_x, wave_y, wave_z])),
        green_stress(first, unit([flip_x, flip_y, flip_z])),
        green_stress(second, unit([wave_x, edge_y, wave_z])),
        green_stress(second, unit([flip_x, -edge_y, flip_z])),
    ]
    result = [0.5 * ((parts[0][k] + parts[1][k]) + (parts[2][k] + parts[3][k])) for k in range(COMPS)]

    high, low = split(jnp.concatenate(result, axis=0))
    inverse = table[512:640, 384:]
    value = mul(high, inverse, PLAIN) + mul(low, inverse, PLAIN)
    value = (value.reshape(6, 32, 128) * cosine - turned(value).reshape(6, 32, 128) * sine).reshape(192, 128)
    stacked = jnp.concatenate([value, turned(value)], axis=0)
    answer = dot3((table[384:640, :384], table[640:896, :384]), split(stacked))
    kind = lax.broadcasted_iota(jnp.int32, (256, 128), 0) % 8
    answer = jnp.where(kind == 6, rows, answer).reshape(32, 8, 128)
    for copy in range(out_ref.shape[1]):
        out_ref[:, copy] = answer


def local_kernel(orient_ref, kappa_ref, phase_ref, part_ref):
    step = pl.program_id(0)
    per_step = phase_ref.shape[0]
    for index in range(per_step):
        orient = orient_ref[step * per_step + index]
        kappa = [TIME_STEP * kappa_ref[d, orient] for d in range(3)]
        center = 1.0 - 2.0 * (kappa[0] + kappa[1] + kappa[2])
        for x in range(SLAB):
            p = phase_ref[index, x]
            if x == 0:
                beside = phase_ref[index, x + 1]
            elif x == SLAB - 1:
                beside = phase_ref[index, x - 1]
            else:
                beside = phase_ref[index, x - 1] + phase_ref[index, x + 1]
            moved = kappa[0] * beside
            moved = moved + kappa[1] * (pltpu.roll(p, 1, 0) + pltpu.roll(p, NY - 1, 0))
            moved = moved + kappa[2] * (pltpu.roll(p, 1, 1) + pltpu.roll(p, NZ - 1, 1))
            cubic = (6.0 * TIME_STEP) - (TIME_STEP * (4.0 - 2.0 * CROSS_COUPLING)) * p
            part_ref[index, x] = p * (center + p * cubic) + moved


def edges_kernel(place_ref, orient_ref, kappa_ref, *refs):
    planes, (low_out, high_out) = refs[:8], refs[8:]
    x = place_ref[2]
    direct = (x != 0, x != SLAB - 1)
    half = planes[0].shape[0]
    for variant in range(2 * half):
        kappa = TIME_STEP * kappa_ref[0, orient_ref[variant]]
        for side, out in enumerate((low_out, high_out)):
            near, relayed = planes[side * 4 + variant // half], planes[side * 4 + 2 + variant // half]
            out[variant] = kappa * jnp.where(direct[side], near[variant % half], relayed[variant % half])


def update_kernel(
    place_ref, family_ref, eps_ref, mine_ref, other_ref, table, phase_ref, low_hbm, high_hbm, part_hbm,
    next_ref, stress_ref, base, low_ref, high_ref, part_ref, sems,
):
    step = pl.program_id(0)
    per_step = next_ref.shape[0]

    def part_copy(index):
        rows = pl.ds(index * per_step, per_step)
        return pltpu.make_async_copy(part_hbm.at[rows], part_ref.at[rows], sems.at[index])

    edge_copies = [
        pltpu.make_async_copy(low_hbm, low_ref, sems.at[phase_ref.shape[0] // per_step]),
        pltpu.make_async_copy(high_hbm, high_ref, sems.at[phase_ref.shape[0] // per_step + 1]),
    ]

    @pl.when(step == 0)
    def _():
        for copy in edge_copies:
            copy.start()
        for index in range(phase_ref.shape[0] // per_step):
            part_copy(index).start()
        first = place_ref[0] == 0

        def line(k):
            mine = mine_ref[pl.ds(k, 128, stride=8), :]
            other = other_ref[pl.ds(k, 128, stride=8), :]
            return jnp.concatenate([jnp.where(first, mine, other), jnp.where(first, other, mine)], axis=1)

        lines = [line(k) for k in range(COMPS)]
        packed = dot3(split(jnp.concatenate([block[:8] for block in lines], axis=0)), (table[2], table[3]))
        along_y = dot3(split(jnp.concatenate(lines, axis=0)), (table[0], table[1]))
        top = lax.broadcasted_iota(jnp.int32, (8, 256), 0) == 0
        for k in range(COMPS):
            block = along_y[k * 128 : k * 128 + 128]
            head = jnp.where(top, packed[k * 8 : k * 8 + 8], block[:8])
            block = jnp.concatenate([head, block[8:]], axis=0)
            block = jnp.concatenate([block[:, :128], block[:, 128:]], axis=0)
            cells = dot3(split(block.T), (table[4], table[5]))
            stress_ref[k] = cells.reshape(SLAB, NY, NZ)
        base[...] = (TIME_STEP * (2.0 + 2.0 * CROSS_COUPLING * line(6))).reshape(SLAB, NY, NZ)
        for copy in edge_copies:
            copy.wait()

    part_copy(step).wait()
    for index in range(per_step):
        variant = step * per_step + index
        family = family_ref[variant]
        weight = [eps_ref[k, family] * (-TIME_STEP * (2.0 if k < 3 else 4.0)) for k in range(COMPS)]
        for x in range(SLAB):
            slope = base[x]
            for k in range(COMPS):
                slope = slope + weight[k] * stress_ref[k, x]
            value = part_ref[variant, x] - phase_ref[variant, x] * slope
            if x == 0:
                value = value + low_ref[variant]
            if x == SLAB - 1:
                value = value + high_ref[variant]
            next_ref[index, x] = value


def vmem():
    return pl.BlockSpec(memory_space=pltpu.VMEM)


def smem():
    return pl.BlockSpec(memory_space=pltpu.SMEM)


def device(x, y, z, core):
    return (y % 4 * 2 + z % 8 // 4) * 32 + x % 4 * 8 + z % 4 * 2 + core


def halo_routes(side, turn):
    first, second = [], []
    for y in range(4):
        for z in range(8):
            for core in range(2):
                for x in range(4):
                    if 0 <= x + side < 4:
                        target = device(x + side, y, z, core)
                    else:
                        row = y + (z >= 4) if side > 0 else y - (z < 4)
                        target = device(x + side, row, z + 3 * turn, core)
                    first.append((device(x, y, z, core), target))
                edge = 0 if side > 0 else 3
                second.append((device(edge, y, z, core), device(edge, y, z + turn, core)))
    return first, second


def limit(mib):
    return pltpu.CompilerParams(vmem_limit_bytes=mib << 20)


def step(phase_field, kappa_table, eps_table, orient_index, family_index):
    slabs = lax.axis_size("gx")
    groups = lax.axis_size("vert")
    runs = groups // 2
    variants = phase_field.shape[0]
    place = lax.axis_index("vert")
    core = (place % 2).astype(jnp.int32)
    kz_own = (lax.axis_index("gx") * runs + place // 2).astype(jnp.int32)
    place_arr = jnp.stack([core, kz_own, (lax.axis_index("gx") % SLAB).astype(jnp.int32)])
    eps_t, kappa_t = eps_table.T, kappa_table.T

    tz = z_table()
    ry, rp = y_tables()
    hbm = pl.BlockSpec(memory_space=pltpu.HBM)

    spread = jax.ShapeDtypeStruct((1024, 128), F32)
    plane = jax.ShapeDtypeStruct((variants // 2, NY, NZ), F32)
    keep, send, *planes = pl.pallas_call(
        sums_kernel,
        in_specs=[smem()] * 3 + [hbm] * 2,
        out_specs=[vmem()] * 6,
        out_shape=[spread] * 2 + [plane] * 4,
        scratch_shapes=[
            pltpu.VMEM(phase_field.shape, F32),
            pltpu.VMEM((6, 256, 256), BF16),
            pltpu.VMEM((COMPS * 128, NZ), F32),
            pltpu.VMEM((128, NZ), F32),
            pltpu.SemaphoreType.DMA((SLAB + 1,)),
        ],
        compiler_params=limit(24),
        cost_estimate=pl.CostEstimate(flops=10**8, bytes_accessed=9 << 20, transcendentals=0),
        name="sums",
    )(
        place_arr, family_index, eps_t, pltpu.with_memory_space_constraint(phase_field, pltpu.HBM),
        pltpu.with_memory_space_constraint(stacked_halves(tz, ry, rp), pltpu.HBM),
    )

    partner = [(i, i ^ 1) for i in range(groups)]
    same_core = [[g * groups + 2 * r + c for g in range(slabs) for r in range(runs)] for c in range(2)]

    def exchange(value):
        return lax.all_to_all(
            value, ("gx", "vert"), split_axis=0, concat_axis=0, axis_index_groups=same_core, tiled=True
        )

    received = lax.ppermute(send, "vert", partner)
    summed = keep + received
    both = ("gx", "vert")
    arrivals, relays = [], []
    for index, (side, turn) in enumerate(((1, 1), (1, -1), (-1, 1), (-1, -1))):
        first, second = halo_routes(side, turn)
        arrivals.append(lax.ppermute(planes[index], both, first))
        relays.append(lax.ppermute(arrivals[index], both, second))

    arrived = exchange(summed.reshape(128, 8, 128)).reshape(slabs, runs, 8, 128)

    answers = pl.pallas_call(
        spectral_kernel,
        in_specs=[smem()] + [vmem()] * 2,
        out_specs=vmem(),
        out_shape=jax.ShapeDtypeStruct((slabs, runs, 8, 128), F32),
        compiler_params=limit(12),
        cost_estimate=pl.CostEstimate(flops=10**8, bytes_accessed=4 << 20, transcendentals=0),
        name="spectral",
    )(place_arr, arrived, spectral_tables(*x_tables()))

    mine = exchange(answers.reshape(128, 8, 128)).reshape(1024, 128)
    other = lax.ppermute(mine, "vert", partner)

    edge_low, edge_high = pl.pallas_call(
        edges_kernel,
        in_specs=[smem()] * 3 + [vmem()] * 8,
        out_specs=[vmem()] * 2,
        out_shape=[jax.ShapeDtypeStruct((variants, NY, NZ), F32)] * 2,
        compiler_params=limit(4),
        cost_estimate=pl.CostEstimate(flops=10**6, bytes_accessed=3 << 20, transcendentals=0),
        name="edges",
    )(place_arr, orient_index, kappa_t, *arrivals[:2], *relays[:2], *arrivals[2:], *relays[2:])

    per_step = 2
    whole = pl.BlockSpec((per_step, SLAB, NY, NZ), lambda i: (i, 0, 0, 0))
    part = pl.pallas_call(
        local_kernel,
        grid=(variants // per_step,),
        in_specs=[smem()] * 2 + [whole],
        out_specs=whole,
        out_shape=jax.ShapeDtypeStruct(phase_field.shape, F32),
        compiler_params=limit(4),
        cost_estimate=pl.CostEstimate(flops=10**7, bytes_accessed=20 << 20, transcendentals=0),
        name="local",
    )(orient_index, kappa_t, pltpu.with_memory_space_constraint(phase_field, pltpu.HBM))

    phase_next, stress = pl.pallas_call(
        update_kernel,
        grid=(variants // per_step,),
        in_specs=[smem()] * 3 + [vmem()] * 4 + [hbm] * 3,
        out_specs=[whole, pl.BlockSpec((COMPS, SLAB, NY, NZ), lambda i: (0, 0, 0, 0))],
        out_shape=[
            jax.ShapeDtypeStruct(phase_field.shape, F32),
            jax.ShapeDtypeStruct((COMPS, SLAB, NY, NZ), F32),
        ],
        scratch_shapes=[
            pltpu.VMEM((SLAB, NY, NZ), F32),
            pltpu.VMEM((variants, NY, NZ), F32),
            pltpu.VMEM((variants, NY, NZ), F32),
            pltpu.VMEM(phase_field.shape, F32),
            pltpu.SemaphoreType.DMA((variants // per_step + 2,)),
        ],
        compiler_params=limit(26),
        cost_estimate=pl.CostEstimate(flops=10**8, bytes_accessed=12 << 20, transcendentals=0),
        name="update",
    )(
        place_arr, family_index, eps_t, mine, other,
        stacked_halves(np.linalg.inv(ry), np.linalg.inv(rp), np.linalg.inv(tz).T),
        phase_field, *(pltpu.with_memory_space_constraint(value, pltpu.HBM) for value in (edge_low, edge_high, part)),
    )
    return phase_next, stress


def solution(mesh):
    return jax.shard_map(
        step,
        mesh=mesh,
        in_specs=(P("vert", "gx", None, None), P(), P(), P("vert"), P("vert")),
        out_specs=(P("vert", "gx", None, None), P(None, "gx", None, None)),
        check_vma=False,
    )
```

time: 111 us -> 112 us (level); the launches traced: 111 us -> 110 us
  blocking collectives: 0 us -> 35.2 us
  waiting for transfers between devices: 52.5 us -> 23.2 us
  starting transfers between devices: 31.2 us -> 27.1 us
  other arithmetic: 2.52 us -> 0.13 us
  local copies, waits for them, and re-layouts: 5.45 us -> 4.28 us
    all_to_all x0 -> x1, blocking collectives: none -> 35.2 us  [exchange(): lax.all_to_all(value, ('gx', 'vert'), split_axis=0, concat_axis=0, axis_i...]
    all_to_all x2 -> x1, waiting for transfers between devices: 29.2 us -> 9.47 us  [exchange(): lax.all_to_all(value, ('gx', 'vert'), split_axis=0, concat_axis=0, axis_i...]
    all_to_all x2 -> x1, starting transfers between devices: 21.7 us -> 6.55 us  [exchange(): lax.all_to_all(value, ('gx', 'vert'), split_axis=0, concat_axis=0, axis_i...]
    ppermute x4 -> x10, starting transfers between devices: 9.55 us -> 20.6 us  [the longest x4 11.7 us: step(): arrivals.append(lax.ppermute(planes[index], both, first))]
    ppermute x4 -> x10, waiting for transfers between devices: 23.2 us -> 13.7 us  [the longest x4 11.8 us: step(): arrivals.append(lax.ppermute(planes[index], both, first))]
    reshape x1, other arithmetic: 1.91 us -> 0.05 us  [step(): arrived = exchange(summed.reshape(128, 8, 128)).reshape(slabs, runs, 8, 128)]
    pallas_call x3 -> x5, Pallas kernels: 18.4 us -> 18.9 us  [the longest x1 5.98 us: step(): pl.pallas_call(update_kernel, grid=(variants // per_step,), in_specs=[sme...]
    unnamed x16 -> x24, local copies, waits for them, and re-layouts: 4.56 us -> 4.28 us
  transfers between devices with their start and end apart: 6 -> 11, of which waited for: 5 -> 3; matrix products, arithmetic and copies ran while one was open for 2% -> 0% of each run, Pallas kernels for 0% -> 5%
where the time goes in v1:
time: 112 us; the launch traced here: 110 us
  blocking collectives  35.2 us (31%)
  starting transfers between devices  27.1 us (24%)
  waiting for transfers between devices  23.2 us (21%)
  Pallas kernels  18.9 us (17%)
  local copies, waits for them, and re-layouts  4.28 us (4%)
    all_to_all x1, blocking collectives, exchange(): lax.all_to_all(value, ('gx', 'vert'), split_axis=0, concat_axis=0, axis_i...  35.2 us
    ppermute x4, waiting for transfers between devices, step(): arrivals.append(lax.ppermute(planes[index], both, first))  11.8 us
    ppermute x4, starting transfers between devices, step(): arrivals.append(lax.ppermute(planes[index], both, first))  11.7 us
    all_to_all x1, waiting for transfers between devices, exchange(): lax.all_to_all(value, ('gx', 'vert'), split_axis=0, concat_axis=0, axis_i...  9.47 us
    ppermute x4, starting transfers between devices, step(): relays.append(lax.ppermute(arrivals[index], both, second))  8.75 us
    all_to_all x1, starting transfers between devices, exchange(): lax.all_to_all(value, ('gx', 'vert'), split_axis=0, concat_axis=0, axis_i...  6.55 us
    pallas_call x1, Pallas kernels, step(): pl.pallas_call(update_kernel, grid=(variants // per_step,), in_specs=[sme...  5.98 us
    pallas_call x1, Pallas kernels, step(): pl.pallas_call(local_kernel, grid=(variants // per_step,), in_specs=[smem...  5.1 us
  transfers between devices with their start and end apart: 11, of which 3 were waited for; matrix products, arithmetic and copies ran while one was open for 0% of the time, Pallas kernels for 5%

profile of v1, /device:TPU:32, one launch (start us, length us, event | category | flops | bytes accessed | tf_op | source)
XLA Modules:
  0.0 109.7 jit_solution(9683967673269413076)
XLA Ops:
  0.7 0.1 pad_add_fusion.place_ref
  0.7 0.0 copy-start.6
  0.7 0.7 copy-done.6
  1.4 0.7 copy-done.10
  2.1 4.2 %sums.1 = (f32[1024,128]{1,0:T(8,128)S(1)}, f32[1024,128]{1,0:T(8,128)S(1)}, f32[8,32,256]{2,1,0:T(8,128)S(1)}, f32[8,32,256]{2,1,0:T(8,128)S(1)}, f32[8,32,256]{2,1,0:T(8,128)S(1)}, /*index=5*/f32[8,32,256]{2,1,0:T(8,128)S(1)}) custom-call(s32[3]{0:T(128)S(1)} %pad_add_fusion.place_ref, s32[16]{0:T(128)S(1)} %copy-done.10, f32[6,12]{1,0:T(8,128)S(1)} %bitcast.13, ...), custom_call_target="tpu_custom_call" | custom-call | flops 100000000 | bytes 9437184 | tf_op jit(solution)/shard_map/sums/pallas_call | solution.py:421
  6.3 0.1 collective-permute-start
  6.4 1.9 %collective-permute-done = f32[1024,128]{1,0:T(8,128)S(1)} collective-permute-done((f32[1024,128]{1,0:T(8,128)S(1)}, f32[1024,128]{1,0:T(8,128)S(1)}, u32[]{:S(2)}, u32[]{:S(2)}) %collective-permute-start) | collective-permute-done | bytes 524320 | tf_op jit(solution)/shard_map/ppermute | solution.py:449
  8.3 0.1 add_bitcast_fusion
  8.3 0.0 copy-start.8
  8.3 0.0 copy-start.9
  8.3 35.2 %all_to_all.10 = f32[128,8,128]{2,1,0:T(8,128)S(1)} all-to-all(f32[128,8,128]{2,1,0:T(8,128)S(1)} %add_bitcast_fusion), channel_id=1, replica_groups={{0,2,4,6,8,10,12,14,16,18,20,22,24,26,28,30,32,34,36,38,40,42,44,46,48,..., dimensions={0} | all-to-all | bytes 1048576 | tf_op jit(solution)/shard_map/all_to_all | solution.py:445
  43.6 0.0 copy-done.2
  43.6 3.0 %spectral.1 = f32[32,4,8,128]{3,2,1,0:T(8,128)} custom-call(s32[3]{0:T(128)S(1)} %pad_add_fusion.place_ref, f32[32,4,8,128]{3,2,1,0:T(8,128)S(1)} %bitcast.12, bf16[896,512]{1,0:T(8,128)(2,1)S(1)} %copy-done.2), custom_call_target="tpu_custom_call" | custom-call | flops 100000000 | bytes 4194304 | tf_op jit(solution)/shard_map/spectral/pallas_call | solution.py:460
  46.5 6.6 %all-to-all-start.1 = ((f32[128,8,128]{2,1,0:T(8,128)}), f32[128,8,128]{2,1,0:T(8,128)S(1)}, u32[]{:S(2)}, u32[]{:S(2)}) async-start(f32[128,8,128]{2,1,0:T(8,128)} %bitcast.6), calls=%async_computation.1 | async-start | bytes 1048576 | tf_op jit(solution)/shard_map/all_to_all | solution.py:445
  53.1 1.6 %collective-permute-start.2 = (f32[8,32,256]{2,1,0:T(8,128)S(1)}, f32[8,32,256]{2,1,0:T(8,128)S(1)}, u32[]{:S(2)}, u32[]{:S(2)}) collective-permute-start(f32[8,32,256]{2,1,0:T(8,128)S(1)} %get-tuple-element.12), channel_id=1, source_target_pairs={{0,8},{8,16},{16,24},{24,6},{1,9},{9,17},{17,25},{25,7},{2,10},{10... | collective-permute-start | bytes 786440 | tf_op jit(solution)/shard_map/ppermute | solution.py:455
  54.6 1.5 %collective-permute-start.3 = (f32[8,32,256]{2,1,0:T(8,128)S(1)}, f32[8,32,256]{2,1,0:T(8,128)S(1)}, u32[]{:S(2)}, u32[]{:S(2)}) collective-permute-start(f32[8,32,256]{2,1,0:T(8,128)S(1)} %get-tuple-element.13), channel_id=1, source_target_pairs={{0,8},{8,16},{16,24},{24,34},{1,9},{9,17},{17,25},{25,35},{2,10},{... | collective-permute-start | bytes 786440 | tf_op jit(solution)/shard_map/ppermute | solution.py:455
  56.1 7.8 %collective-permute-start.6 = (f32[8,32,256]{2,1,0:T(8,128)S(1)}, f32[8,32,256]{2,1,0:T(8,128)S(1)}, u32[]{:S(2)}, u32[]{:S(2)}) collective-permute-start(f32[8,32,256]{2,1,0:T(8,128)S(1)} %get-tuple-element.14), channel_id=1, source_target_pairs={{0,222},{8,0},{16,8},{24,16},{1,223},{9,1},{17,9},{25,17},{2,248},... | collective-permute-start | bytes 786440 | tf_op jit(solution)/shard_map/ppermute | solution.py:455
  63.9 0.9 collective-permute-start.7
  64.8 9.5 %all-to-all-done.1 = f32[128,8,128]{2,1,0:T(8,128)S(1)} async-done(((f32[128,8,128]{2,1,0:T(8,128)}), f32[128,8,128]{2,1,0:T(8,128)S(1)}, u32[]{:S(2)}, u32[]{:S(2)}) %all-to-all-start.1) | async-done | bytes 524320 | tf_op jit(solution)/shard_map/all_to_all | solution.py:445
  74.3 0.0 collective-permute-start.1
  74.3 11.8 %collective-permute-done.2.refs_0_ = f32[8,32,256]{2,1,0:T(8,128)S(1)} collective-permute-done((f32[8,32,256]{2,1,0:T(8,128)S(1)}, f32[8,32,256]{2,1,0:T(8,128)S(1)}, u32[]{:S(2)}, u32[]{:S(2)}) %collective-permute-start.2) | collective-permute-done | bytes 262176 | tf_op jit(solution)/shard_map/ppermute | solution.py:455
  86.1 4.0 %collective-permute-start.4 = (f32[8,32,256]{2,1,0:T(8,128)S(1)}, f32[8,32,256]{2,1,0:T(8,128)S(1)}, u32[]{:S(2)}, u32[]{:S(2)}) collective-permute-start(f32[8,32,256]{2,1,0:T(8,128)S(1)} %collective-permute-done.2.refs_0_), channel_id=1, source_target_pairs={{0,2},{1,3},{2,4},{3,5},{4,6},{5,7},{6,32},{7,33},{32,34},{33,35},... | collective-permute-start | bytes 786440 | tf_op jit(solution)/shard_map/ppermute | solution.py:456
  90.1 0.0 collective-permute-done.3.refs_1_
  90.1 3.4 %collective-permute-start.5 = (f32[8,32,256]{2,1,0:T(8,128)S(1)}, f32[8,32,256]{2,1,0:T(8,128)S(1)}, u32[]{:S(2)}, u32[]{:S(2)}) collective-permute-start(f32[8,32,256]{2,1,0:T(8,128)S(1)} %collective-permute-done.3.refs_1_), channel_id=1, source_target_pairs={{0,38},{1,39},{2,0},{3,1},{4,2},{5,3},{6,4},{7,5},{32,6},{33,7},{3... | collective-permute-start | bytes 786440 | tf_op jit(solution)/shard_map/ppermute | solution.py:456
  93.5 0.0 collective-permute-done.6.refs_4_
  93.5 0.7 collective-permute-start.8
  94.2 0.0 collective-permute-done.7.refs_5_
  94.2 0.7 collective-permute-start.9
  94.9 0.0 copy-done.8
  94.9 0.0 copy-done.9
  94.9 0.0 copy-start.3
  94.9 5.1 %local.1.part_hbm = f32[16,4,32,256]{3,2,1,0:T(8,128)S(1)} custom-call(s32[16]{0:T(128)S(1)} %copy-done.9, f32[3,24]{1,0:T(4,128)S(1)} %bitcast.15, f32[16,4,32,256]{3,2,1,0:T(8,128)} %phase_ref.3), custom_call_target="tpu_custom_call" | custom-call | flops 10000000 | bytes 20971520 | tf_op jit(solution)/shard_map/local/pallas_call | solution.py:485
  100.0 0.0 copy-start.1
  100.1 1.3 %copy-done.1 = f32[16,4,32,256]{3,2,1,0:T(8,128)} copy-done((f32[16,4,32,256]{3,2,1,0:T(8,128)}, f32[16,4,32,256]{3,2,1,0:T(8,128)S(1)}, u32[]{:S(2)}) %copy-start.1) | copy-done | bytes 2097176
  101.4 0.0 collective-permute-done.4.refs_2_
  101.4 0.0 collective-permute-done.5.refs_3_
  101.4 0.0 collective-permute-done.8.refs_6_
  101.4 0.0 collective-permute-done.9.refs_7_
  101.4 0.7 edges.1
  102.1 0.0 copy-start.4
  102.1 0.8 copy-done.4
  102.9 0.8 copy-done.5
  103.7 0.0 collective-permute-done.1.other_ref
  103.7 0.0 copy-done.3
  103.7 0.0 copy-done
  103.7 0.0 copy-done.7
  103.7 0.0 copy-done.11
  103.7 6.0 %update.1 = (f32[16,4,32,256]{3,2,1,0:T(8,128)}, f32[6,4,32,256]{3,2,1,0:T(8,128)}) custom-call(s32[3]{0:T(128)S(1)} %pad_add_fusion.place_ref, s32[16]{0:T(128)S(1)} %copy-done.11, f32[6,12]{1,0:T(8,128)S(1)} %bitcast.14, f32[1024,128]{1,0:T(8,128)S(1)} %bitcast.11, f32[1024,128]{1,0:T(8,128)S(1)} %collective-permute-done.1.other_ref, ...), custom_call_target="tpu_custom_call" | custom-call | flops 100000000 | bytes 12582912 | tf_op jit(solution)/shard_map/update/pallas_call | solution.py:496
  (6 shorter events, 0.0 us)
Async XLA Ops:
  0.7 0.7 copy-start.6
  1.4 0.7 copy-start.10
  2.1 41.5 %copy-start.2 = (bf16[896,512]{1,0:T(8,128)(2,1)S(1)}, bf16[896,512]{1,0:T(8,128)(2,1)}, u32[]{:S(2)}) copy-start(bf16[896,512]{1,0:T(8,128)(2,1)} %constant.50.clone.table) | copy-start | bytes 2752516
  6.3 2.0 %collective-permute-start = (f32[1024,128]{1,0:T(8,128)S(1)}, f32[1024,128]{1,0:T(8,128)S(1)}, u32[]{:S(2)}, u32[]{:S(2)}) collective-permute-start(f32[1024,128]{1,0:T(8,128)S(1)} %get-tuple-element.11), channel_id=1, source_target_pairs={{0,1},{1,0},{2,3},{3,2},{4,5},{5,4},{6,7},{7,6},{8,9},{9,8},{10,11... | collective-permute-start | bytes 1572872 | tf_op jit(solution)/shard_map/ppermute | solution.py:449
  8.3 86.6 %copy-start.8 = (f32[24,3]{0,1:T(4,128)S(1)}, f32[24,3]{0,1:T(4,128)}, u32[]{:S(2)}) copy-start(f32[24,3]{0,1:T(4,128)} %param.9) | copy-start | bytes 868
  8.3 86.6 %copy-start.9 = (s32[16]{0:T(128)S(1)}, s32[16]{0:T(128)}, u32[]{:S(2)}) copy-start(s32[16]{0:T(128)} %orient_ref.3) | copy-start | bytes 196
  46.5 27.8 %all-to-all-start.1 = ((f32[128,8,128]{2,1,0:T(8,128)}), f32[128,8,128]{2,1,0:T(8,128)S(1)}, u32[]{:S(2)}, u32[]{:S(2)}) async-start(f32[128,8,128]{2,1,0:T(8,128)} %bitcast.6), calls=%async_computation.1 | async-start | bytes 1048576 | tf_op jit(solution)/shard_map/all_to_all | solution.py:445
  53.1 33.0 %collective-permute-start.2 = (f32[8,32,256]{2,1,0:T(8,128)S(1)}, f32[8,32,256]{2,1,0:T(8,128)S(1)}, u32[]{:S(2)}, u32[]{:S(2)}) collective-permute-start(f32[8,32,256]{2,1,0:T(8,128)S(1)} %get-tuple-element.12), channel_id=1, source_target_pairs={{0,8},{8,16},{16,24},{24,6},{1,9},{9,17},{17,25},{25,7},{2,10},{10... | collective-permute-start | bytes 786440 | tf_op jit(solution)/shard_map/ppermute | solution.py:455
  54.6 35.4 %collective-permute-start.3 = (f32[8,32,256]{2,1,0:T(8,128)S(1)}, f32[8,32,256]{2,1,0:T(8,128)S(1)}, u32[]{:S(2)}, u32[]{:S(2)}) collective-permute-start(f32[8,32,256]{2,1,0:T(8,128)S(1)} %get-tuple-element.13), channel_id=1, source_target_pairs={{0,8},{8,16},{16,24},{24,34},{1,9},{9,17},{17,25},{25,35},{2,10},{... | collective-permute-start | bytes 786440 | tf_op jit(solution)/shard_map/ppermute | solution.py:455
  56.1 37.4 %collective-permute-start.6 = (f32[8,32,256]{2,1,0:T(8,128)S(1)}, f32[8,32,256]{2,1,0:T(8,128)S(1)}, u32[]{:S(2)}, u32[]{:S(2)}) collective-permute-start(f32[8,32,256]{2,1,0:T(8,128)S(1)} %get-tuple-element.14), channel_id=1, source_target_pairs={{0,222},{8,0},{16,8},{24,16},{1,223},{9,1},{17,9},{25,17},{2,248},... | collective-permute-start | bytes 786440 | tf_op jit(solution)/shard_map/ppermute | solution.py:455
  63.9 30.3 %collective-permute-start.7 = (f32[8,32,256]{2,1,0:T(8,128)S(1)}, f32[8,32,256]{2,1,0:T(8,128)S(1)}, u32[]{:S(2)}, u32[]{:S(2)}) collective-permute-start(f32[8,32,256]{2,1,0:T(8,128)S(1)} %get-tuple-element.15), channel_id=1, source_target_pairs={{0,250},{8,0},{16,8},{24,16},{1,251},{9,1},{17,9},{25,17},{2,252},... | collective-permute-start | bytes 786440 | tf_op jit(solution)/shard_map/ppermute | solution.py:455
  74.3 29.4 %collective-permute-start.1 = (f32[1024,128]{1,0:T(8,128)S(1)}, f32[1024,128]{1,0:T(8,128)S(1)}, u32[]{:S(2)}, u32[]{:S(2)}) collective-permute-start(f32[1024,128]{1,0:T(8,128)S(1)} %bitcast.10), channel_id=1, source_target_pairs={{0,1},{1,0},{2,3},{3,2},{4,5},{5,4},{6,7},{7,6},{8,9},{9,8},{10,11... | collective-permute-start | bytes 1572872 | tf_op jit(solution)/shard_map/ppermute | solution.py:471
  86.1 15.3 %collective-permute-start.4 = (f32[8,32,256]{2,1,0:T(8,128)S(1)}, f32[8,32,256]{2,1,0:T(8,128)S(1)}, u32[]{:S(2)}, u32[]{:S(2)}) collective-permute-start(f32[8,32,256]{2,1,0:T(8,128)S(1)} %collective-permute-done.2.refs_0_), channel_id=1, source_target_pairs={{0,2},{1,3},{2,4},{3,5},{4,6},{5,7},{6,32},{7,33},{32,34},{33,35},... | collective-permute-start | bytes 786440 | tf_op jit(solution)/shard_map/ppermute | solution.py:456
  90.1 11.3 %collective-permute-start.5 = (f32[8,32,256]{2,1,0:T(8,128)S(1)}, f32[8,32,256]{2,1,0:T(8,128)S(1)}, u32[]{:S(2)}, u32[]{:S(2)}) collective-permute-start(f32[8,32,256]{2,1,0:T(8,128)S(1)} %collective-permute-done.3.refs_1_), channel_id=1, source_target_pairs={{0,38},{1,39},{2,0},{3,1},{4,2},{5,3},{6,4},{7,5},{32,6},{33,7},{3... | collective-permute-start | bytes 786440 | tf_op jit(solution)/shard_map/ppermute | solution.py:456
  93.5 7.9 %collective-permute-start.8 = (f32[8,32,256]{2,1,0:T(8,128)S(1)}, f32[8,32,256]{2,1,0:T(8,128)S(1)}, u32[]{:S(2)}, u32[]{:S(2)}) collective-permute-start(f32[8,32,256]{2,1,0:T(8,128)S(1)} %collective-permute-done.6.refs_4_), channel_id=1, source_target_pairs={{24,26},{25,27},{26,28},{27,29},{28,30},{29,31},{30,56},{31,57},{5... | collective-permute-start | bytes 786440 | tf_op jit(solution)/shard_map/ppermute | solution.py:456
  94.2 7.2 %collective-permute-start.9 = (f32[8,32,256]{2,1,0:T(8,128)S(1)}, f32[8,32,256]{2,1,0:T(8,128)S(1)}, u32[]{:S(2)}, u32[]{:S(2)}) collective-permute-start(f32[8,32,256]{2,1,0:T(8,128)S(1)} %collective-permute-done.7.refs_5_), channel_id=1, source_target_pairs={{24,62},{25,63},{26,24},{27,25},{28,26},{29,27},{30,28},{31,29},{5... | collective-permute-start | bytes 786440 | tf_op jit(solution)/shard_map/ppermute | solution.py:456
  94.9 8.8 %copy-start.3 = (bf16[6,256,256]{2,1,0:T(8,128)(2,1)S(1)}, bf16[6,256,256]{2,1,0:T(8,128)(2,1)}, u32[]{:S(2)}) copy-start(bf16[6,256,256]{2,1,0:T(8,128)(2,1)} %constant.51.clone.table) | copy-start | bytes 2359300
  100.0 1.3 %copy-start.1 = (f32[16,4,32,256]{3,2,1,0:T(8,128)}, f32[16,4,32,256]{3,2,1,0:T(8,128)S(1)}, u32[]{:S(2)}) copy-start(f32[16,4,32,256]{3,2,1,0:T(8,128)S(1)} %local.1.part_hbm) | copy-start | bytes 6291460
  101.4 2.3 %copy-start = (f32[16,4,32,256]{3,2,1,0:T(8,128)S(1)}, f32[16,4,32,256]{3,2,1,0:T(8,128)}, u32[]{:S(2)}) copy-start(f32[16,4,32,256]{3,2,1,0:T(8,128)} %phase_ref.3) | copy-start | bytes 6291460
  101.4 2.3 %copy-start.7 = (f32[12,6]{0,1:T(8,128)S(1)}, f32[12,6]{0,1:T(8,128)}, u32[]{:S(2)}) copy-start(f32[12,6]{0,1:T(8,128)} %param.10) | copy-start | bytes 868
  101.4 2.3 %copy-start.11 = (s32[16]{0:T(128)S(1)}, s32[16]{0:T(128)}, u32[]{:S(2)}) copy-start(s32[16]{0:T(128)} %family_ref.3) | copy-start | bytes 196
  102.1 0.8 copy-start.4
  102.9 0.8 copy-start.5

commit v2 on v1

--- a/solution.py
+++ b/solution.py
@@ -118,14 +118,20 @@
 
 
 def sums_kernel(
-    place_ref, family_ref, eps_ref, phase_hbm, table_hbm,
-    keep_ref, send_ref, last_a, last_b, front_a, front_b, phase, table, eigen, square, sems,
+    place_ref, family_hbm, eps_hbm, phase_hbm, table_hbm,
+    keep_ref, send_ref, last_ref, front_ref, far_ref, relay_ref, phase, table, eigen, square, family_ref, eps_ref, sems,
 ):
     variants = phase.shape[0]
     loads = [pltpu.make_async_copy(phase_hbm.at[:, x], phase.at[:, x], sems.at[x]) for x in range(SLAB)]
     loads.append(pltpu.make_async_copy(table_hbm, table, sems.at[SLAB]))
-    for load in loads:
+    small = [
+        pltpu.make_async_copy(family_hbm, family_ref, sems.at[SLAB + 1]),
+        pltpu.make_async_copy(eps_hbm, eps_ref, sems.at[SLAB + 2]),
+    ]
+    for load in small + loads:
         load.start()
+    for load in small:
+        load.wait()
     weight = [[eps_ref[k, family_ref[v]] for k in range(COMPS)] for v in range(variants)]
     for x in range(SLAB):
         loads[x].wait()
@@ -148,9 +154,11 @@
 
         lax.fori_loop(0, NY // 8, tile_sum, 0)
         if x in (0, SLAB - 1):
-            low_half, high_half = (front_a, front_b) if x == 0 else (last_a, last_b)
-            low_half[...] = phase[: variants // 2, x]
-            high_half[...] = phase[variants // 2 :, x]
+            (front_ref if x == 0 else last_ref)[...] = phase[:, x]
+    forward = place_ref[2] == SLAB - 1
+    for v in range(variants):
+        target = far_ref if v < variants // 2 else relay_ref
+        target[v % (variants // 2)] = jnp.where(forward, phase[v, SLAB - 1], phase[v, 0])
     loads[SLAB].wait()
 
     first = place_ref[0] == 0
@@ -295,40 +303,41 @@
             part_ref[index, x] = p * (center + p * cubic) + moved
 
 
-def edges_kernel(place_ref, orient_ref, kappa_ref, *refs):
-    planes, (low_out, high_out) = refs[:8], refs[8:]
+def edges_kernel(place_ref, orient_ref, kappa_ref, near_low, near_high, far, carried, low_out, high_out):
     x = place_ref[2]
-    direct = (x != 0, x != SLAB - 1)
-    half = planes[0].shape[0]
+    half = far.shape[0]
     for variant in range(2 * half):
         kappa = TIME_STEP * kappa_ref[0, orient_ref[variant]]
-        for side, out in enumerate((low_out, high_out)):
-            near, relayed = planes[side * 4 + variant // half], planes[side * 4 + 2 + variant // half]
-            out[variant] = kappa * jnp.where(direct[side], near[variant % half], relayed[variant % half])
+        remote = (far if variant < half else carried)[variant % half]
+        low_out[variant] = kappa * jnp.where(x == 0, remote, near_low[variant])
+        high_out[variant] = kappa * jnp.where(x == SLAB - 1, remote, near_high[variant])
 
 
 def update_kernel(
-    place_ref, family_ref, eps_ref, mine_ref, other_ref, table, phase_ref, low_hbm, high_hbm, part_hbm,
+    place_ref, family_ref, eps_ref, mine_ref, other_ref, table, phase_ref, low_hbm, high_hbm, part0, part1,
     next_ref, stress_ref, base, low_ref, high_ref, part_ref, sems,
 ):
     step = pl.program_id(0)
     per_step = next_ref.shape[0]
 
-    def part_copy(index):
-        rows = pl.ds(index * per_step, per_step)
-        return pltpu.make_async_copy(part_hbm.at[rows], part_ref.at[rows], sems.at[index])
+    count = phase_ref.shape[0] // per_step
+
+    def part_start(index):
+        source, at = (part0, index) if index < count // 2 else (part1, index - count // 2)
+        rows, target = pl.ds(at * per_step, per_step), pl.ds(index * per_step, per_step)
+        return pltpu.make_async_copy(source.at[rows], part_ref.at[target], sems.at[index])
 
     edge_copies = [
-        pltpu.make_async_copy(low_hbm, low_ref, sems.at[phase_ref.shape[0] // per_step]),
-        pltpu.make_async_copy(high_hbm, high_ref, sems.at[phase_ref.shape[0] // per_step + 1]),
+        pltpu.make_async_copy(low_hbm, low_ref, sems.at[count]),
+        pltpu.make_async_copy(high_hbm, high_ref, sems.at[count + 1]),
     ]
 
     @pl.when(step == 0)
     def _():
         for copy in edge_copies:
             copy.start()
-        for index in range(phase_ref.shape[0] // per_step):
-            part_copy(index).start()
+        for index in range(count):
+            part_start(index).start()
         first = place_ref[0] == 0
 
         def line(k):
@@ -351,7 +360,8 @@
         for copy in edge_copies:
             copy.wait()
 
-    part_copy(step).wait()
+    rows = pl.ds(step * per_step, per_step)
+    pltpu.make_async_copy(part0.at[pl.ds(0, per_step)], part_ref.at[rows], sems.at[step]).wait()
     for index in range(per_step):
         variant = step * per_step + index
         family = family_ref[variant]
@@ -380,21 +390,24 @@
     return (y % 4 * 2 + z % 8 // 4) * 32 + x % 4 * 8 + z % 4 * 2 + core
 
 
-def halo_routes(side, turn):
-    first, second = [], []
+def halo_routes():
+    up, down, far, relay, carry = [], [], [], [], []
     for y in range(4):
         for z in range(8):
             for core in range(2):
-                for x in range(4):
-                    if 0 <= x + side < 4:
-                        target = device(x + side, y, z, core)
-                    else:
-                        row = y + (z >= 4) if side > 0 else y - (z < 4)
-                        target = device(x + side, row, z + 3 * turn, core)
-                    first.append((device(x, y, z, core), target))
-                edge = 0 if side > 0 else 3
-                second.append((device(edge, y, z, core), device(edge, y, z + turn, core)))
-    return first, second
+                here = [device(x, y, z, core) for x in range(4)]
+                after = device(0, y + (z >= 4), z + 4, core)
+                before = device(3, y - (z < 4), z + 4, core)
+                up += [(here[x], here[x + 1]) for x in range(3)]
+                down += [(here[x + 1], here[x]) for x in range(3)]
+                far += [(here[3], after), (here[0], before)]
+                relay += [(here[3], here[2]), (here[0], here[1])]
+                carry += [(here[2], after), (here[1], before)]
+    return up, down, far, relay, carry
+
+
+def in_hbm(value):
+    return pltpu.with_memory_space_constraint(value, pltpu.HBM)
 
 
 def limit(mib):
@@ -416,27 +429,26 @@
     ry, rp = y_tables()
     hbm = pl.BlockSpec(memory_space=pltpu.HBM)
 
+    planes = [jax.ShapeDtypeStruct((count, NY, NZ), F32) for count in (variants, variants // 2)]
     spread = jax.ShapeDtypeStruct((1024, 128), F32)
-    plane = jax.ShapeDtypeStruct((variants // 2, NY, NZ), F32)
-    keep, send, *planes = pl.pallas_call(
+    keep, send, last, front, far, relay = pl.pallas_call(
         sums_kernel,
-        in_specs=[smem()] * 3 + [hbm] * 2,
+        in_specs=[smem()] + [hbm] * 4,
         out_specs=[vmem()] * 6,
-        out_shape=[spread] * 2 + [plane] * 4,
+        out_shape=[spread] * 2 + [planes[0]] * 2 + [planes[1]] * 2,
         scratch_shapes=[
             pltpu.VMEM(phase_field.shape, F32),
             pltpu.VMEM((6, 256, 256), BF16),
             pltpu.VMEM((COMPS * 128, NZ), F32),
             pltpu.VMEM((128, NZ), F32),
-            pltpu.SemaphoreType.DMA((SLAB + 1,)),
+            pltpu.SMEM(family_index.shape, jnp.int32),
+            pltpu.SMEM(eps_t.shape, F32),
+            pltpu.SemaphoreType.DMA((SLAB + 3,)),
         ],
         compiler_params=limit(24),
         cost_estimate=pl.CostEstimate(flops=10**8, bytes_accessed=9 << 20, transcendentals=0),
         name="sums",
-    )(
-        place_arr, family_index, eps_t, pltpu.with_memory_space_constraint(phase_field, pltpu.HBM),
-        pltpu.with_memory_space_constraint(stacked_halves(tz, ry, rp), pltpu.HBM),
-    )
+    )(place_arr, *(in_hbm(value) for value in (family_index, eps_t, phase_field, stacked_halves(tz, ry, rp))))
 
     partner = [(i, i ^ 1) for i in range(groups)]
     same_core = [[g * groups + 2 * r + c for g in range(slabs) for r in range(runs)] for c in range(2)]
@@ -449,11 +461,12 @@
     received = lax.ppermute(send, "vert", partner)
     summed = keep + received
     both = ("gx", "vert")
-    arrivals, relays = [], []
-    for index, (side, turn) in enumerate(((1, 1), (1, -1), (-1, 1), (-1, -1))):
-        first, second = halo_routes(side, turn)
-        arrivals.append(lax.ppermute(planes[index], both, first))
-        relays.append(lax.ppermute(arrivals[index], both, second))
+    up, down, across, handed, carried = halo_routes()
+    relay = lax.ppermute(relay, both, handed)
+    near_low = lax.ppermute(last, both, up)
+    near_high = lax.ppermute(front, both, down)
+    far = lax.ppermute(far, both, across)
+    carry = lax.ppermute(relay, both, carried)
 
     arrived = exchange(summed.reshape(128, 8, 128)).reshape(slabs, runs, 8, 128)
 
@@ -472,31 +485,43 @@
 
     edge_low, edge_high = pl.pallas_call(
         edges_kernel,
-        in_specs=[smem()] * 3 + [vmem()] * 8,
+        in_specs=[smem()] * 3 + [vmem()] * 4,
         out_specs=[vmem()] * 2,
-        out_shape=[jax.ShapeDtypeStruct((variants, NY, NZ), F32)] * 2,
+        out_shape=[pltpu.HBM((variants, NY, NZ), F32)] * 2,
         compiler_params=limit(4),
         cost_estimate=pl.CostEstimate(flops=10**6, bytes_accessed=3 << 20, transcendentals=0),
         name="edges",
-    )(place_arr, orient_index, kappa_t, *arrivals[:2], *relays[:2], *arrivals[2:], *relays[2:])
+    )(place_arr, orient_index, kappa_t, near_low, near_high, far, carry)
 
     per_step = 2
     whole = pl.BlockSpec((per_step, SLAB, NY, NZ), lambda i: (i, 0, 0, 0))
-    part = pl.pallas_call(
-        local_kernel,
-        grid=(variants // per_step,),
-        in_specs=[smem()] * 2 + [whole],
-        out_specs=whole,
-        out_shape=jax.ShapeDtypeStruct(phase_field.shape, F32),
-        compiler_params=limit(4),
-        cost_estimate=pl.CostEstimate(flops=10**7, bytes_accessed=20 << 20, transcendentals=0),
-        name="local",
-    )(orient_index, kappa_t, pltpu.with_memory_space_constraint(phase_field, pltpu.HBM))
+    half = variants // 2
+    orients = [orient_index[:half], orient_index[half:]]
+    part = []
+    for index in range(2):
+        part.append(
+            pl.pallas_call(
+                local_kernel,
+                grid=(half // per_step,),
+                in_specs=[
+                    smem(),
+                    smem(),
+                    pl.BlockSpec(whole.block_shape, lambda i, at=index * half // per_step: (i + at, 0, 0, 0)),
+                ],
+                out_specs=whole,
+                out_shape=pltpu.HBM((half, SLAB, NY, NZ), F32),
+                compiler_params=limit(4),
+                cost_estimate=pl.CostEstimate(flops=10**7, bytes_accessed=10 << 20, transcendentals=0),
+            )(
+                orients[index], kappa_t,
+                in_hbm(phase_field),
+            )
+        )
 
     phase_next, stress = pl.pallas_call(
         update_kernel,
         grid=(variants // per_step,),
-        in_specs=[smem()] * 3 + [vmem()] * 4 + [hbm] * 3,
+        in_specs=[smem()] * 3 + [vmem()] * 4 + [hbm] * 4,
         out_specs=[whole, pl.BlockSpec((COMPS, SLAB, NY, NZ), lambda i: (0, 0, 0, 0))],
         out_shape=[
             jax.ShapeDtypeStruct(phase_field.shape, F32),
@@ -515,7 +540,7 @@
     )(
         place_arr, family_index, eps_t, mine, other,
         stacked_halves(np.linalg.inv(ry), np.linalg.inv(rp), np.linalg.inv(tz).T),
-        phase_field, *(pltpu.with_memory_space_constraint(value, pltpu.HBM) for value in (edge_low, edge_high, part)),
+        phase_field, *(in_hbm(value) for value in (edge_low, edge_high, *part)),
     )
     return phase_next, stress
 

time: 112 us -> 108 us (0.964); the launches traced: 110 us -> 107 us
  starting transfers between devices: 27.1 us -> 17.8 us
  waiting for transfers between devices: 23.2 us -> 30.4 us
  local copies, waits for them, and re-layouts: 4.28 us -> 0.11 us
  Pallas kernels: 18.9 us -> 22.5 us
    ppermute x8 -> x5, starting transfers between devices: 20.5 us -> 11.2 us  [the longest x1 3.83 us: step(): far = lax.ppermute(far, both, across)]
    unnamed x24 -> x14, local copies, waits for them, and re-layouts: 4.28 us -> 0.03 us
    all_to_all x1, waiting for transfers between devices: 9.47 us -> 13.2 us  [exchange(): lax.all_to_all(value, ('gx', 'vert'), split_axis=0, concat_axis=0, axis_i...]
    pallas_call x3 -> x4, Pallas kernels: 9.96 us -> 13.6 us  [the longest x2 7.73 us: step(): pl.pallas_call(local_kernel, grid=(half // per_step,), in_specs=[smem(),...]
    ppermute x8 -> x5, waiting for transfers between devices: 11.8 us -> 15.2 us  [the longest x1 12.7 us: step(): far = lax.ppermute(far, both, across)]
  transfers between devices with their start and end apart: 11 -> 8, of which waited for: 3 -> 4; matrix products, arithmetic and copies ran while one was open for 0% -> 0% of each run, Pallas kernels for 5% -> 9%
where the time goes in v2:
time: 108 us; the launch traced here: 107 us
  blocking collectives  35.2 us (33%)
  waiting for transfers between devices  30.4 us (28%)
  Pallas kernels  22.5 us (21%)
  starting transfers between devices  17.8 us (16%)
    all_to_all x1, blocking collectives, exchange(): lax.all_to_all(value, ('gx', 'vert'), split_axis=0, concat_axis=0, axis_i...  35.2 us
    all_to_all x1, waiting for transfers between devices, exchange(): lax.all_to_all(value, ('gx', 'vert'), split_axis=0, concat_axis=0, axis_i...  13.2 us
    ppermute x1, waiting for transfers between devices, step(): far = lax.ppermute(far, both, across)  12.7 us
    pallas_call x2, Pallas kernels, step(): pl.pallas_call(local_kernel, grid=(half // per_step,), in_specs=[smem(),...  7.73 us
    all_to_all x1, starting transfers between devices, exchange(): lax.all_to_all(value, ('gx', 'vert'), split_axis=0, concat_axis=0, axis_i...  6.55 us
    pallas_call x1, Pallas kernels, step(): pl.pallas_call(update_kernel, grid=(variants // per_step,), in_specs=[sme...  5.99 us
    pallas_call x1, Pallas kernels, step(): pl.pallas_call(sums_kernel, in_specs=[smem()] + [hbm] * 4, out_specs=[vme...  4.18 us
    ppermute x1, starting transfers between devices, step(): far = lax.ppermute(far, both, across)  3.83 us
  transfers between devices with their start and end apart: 8, of which 4 were waited for; matrix products, arithmetic and copies ran while one was open for 0% of the time, Pallas kernels for 9%

profile of v2, /device:TPU:32, one launch (start us, length us, event | category | flops | bytes accessed | tf_op | source)
XLA Modules:
  0.0 107.0 jit_solution(15957628877200402426)
XLA Ops:
  0.7 0.1 pad_add_fusion.place_ref
  0.7 0.0 copy-start.1
  0.7 4.2 %sums.1 = (f32[1024,128]{1,0:T(8,128)S(1)}, f32[1024,128]{1,0:T(8,128)S(1)}, f32[16,32,256]{2,1,0:T(8,128)S(1)}, f32[16,32,256]{2,1,0:T(8,128)S(1)}, f32[8,32,25...) custom-call(s32[3]{0:T(128)S(1)} %pad_add_fusion.place_ref, s32[16]{0:T(128)} %family_ref.1, f32[6,12]{1,0:T(8,128)} %bitcast.16, ...), custom_call_target="tpu_custom_call" | custom-call | flops 100000000 | bytes 9437184 | tf_op jit(solution)/shard_map/sums/pallas_call | solution.py:434
  4.9 0.1 collective-permute-start
  5.0 1.9 %collective-permute-done = f32[1024,128]{1,0:T(8,128)S(1)} collective-permute-done((f32[1024,128]{1,0:T(8,128)S(1)}, f32[1024,128]{1,0:T(8,128)S(1)}, u32[]{:S(2)}, u32[]{:S(2)}) %collective-permute-start) | collective-permute-done | bytes 524320 | tf_op jit(solution)/shard_map/ppermute | solution.py:461
  6.9 0.1 add_bitcast_fusion
  7.0 0.0 copy-start.5
  7.0 0.0 copy-start.3
  7.0 35.2 %all_to_all.10 = f32[128,8,128]{2,1,0:T(8,128)S(1)} all-to-all(f32[128,8,128]{2,1,0:T(8,128)S(1)} %add_bitcast_fusion), channel_id=1, replica_groups={{0,2,4,6,8,10,12,14,16,18,20,22,24,26,28,30,32,34,36,38,40,42,44,46,48,..., dimensions={0} | all-to-all | bytes 1048576 | tf_op jit(solution)/shard_map/all_to_all | solution.py:457
  42.2 0.0 copy-done.1
  42.2 3.0 %spectral.1 = f32[32,4,8,128]{3,2,1,0:T(8,128)} custom-call(s32[3]{0:T(128)S(1)} %pad_add_fusion.place_ref, f32[32,4,8,128]{3,2,1,0:T(8,128)S(1)} %bitcast.12, bf16[896,512]{1,0:T(8,128)(2,1)S(1)} %copy-done.1), custom_call_target="tpu_custom_call" | custom-call | flops 100000000 | bytes 4194304 | tf_op jit(solution)/shard_map/spectral/pallas_call | solution.py:473
  45.2 6.6 %all-to-all-start.1 = ((f32[128,8,128]{2,1,0:T(8,128)}), f32[128,8,128]{2,1,0:T(8,128)S(1)}, u32[]{:S(2)}, u32[]{:S(2)}) async-start(f32[128,8,128]{2,1,0:T(8,128)} %bitcast.6), calls=%async_computation.1 | async-start | bytes 1048576 | tf_op jit(solution)/shard_map/all_to_all | solution.py:457
  51.8 3.4 %collective-permute-start.5 = (f32[8,32,256]{2,1,0:T(8,128)S(1)}, f32[8,32,256]{2,1,0:T(8,128)S(1)}, u32[]{:S(2)}, u32[]{:S(2)}) collective-permute-start(f32[8,32,256]{2,1,0:T(8,128)S(1)} %get-tuple-element.15), channel_id=1, source_target_pairs={{24,16},{0,8},{25,17},{1,9},{26,18},{2,10},{27,19},{3,11},{28,20},... | collective-permute-start | bytes 786440 | tf_op jit(solution)/shard_map/ppermute | solution.py:465
  55.2 1.3 %collective-permute-start.2 = (f32[16,32,256]{2,1,0:T(8,128)S(1)}, f32[16,32,256]{2,1,0:T(8,128)S(1)}, u32[]{:S(2)}, u32[]{:S(2)}) collective-permute-start(f32[16,32,256]{2,1,0:T(8,128)S(1)} %get-tuple-element.12), channel_id=1, source_target_pairs={{0,8},{8,16},{16,24},{1,9},{9,17},{17,25},{2,10},{10,18},{18,26},{... | collective-permute-start | bytes 1572872 | tf_op jit(solution)/shard_map/ppermute | solution.py:466
  56.5 1.3 %collective-permute-start.3 = (f32[16,32,256]{2,1,0:T(8,128)S(1)}, f32[16,32,256]{2,1,0:T(8,128)S(1)}, u32[]{:S(2)}, u32[]{:S(2)}) collective-permute-start(f32[16,32,256]{2,1,0:T(8,128)S(1)} %get-tuple-element.13), channel_id=1, source_target_pairs={{8,0},{16,8},{24,16},{9,1},{17,9},{25,17},{10,2},{18,10},{26,18},{... | collective-permute-start | bytes 1572872 | tf_op jit(solution)/shard_map/ppermute | solution.py:467
  57.8 13.2 %all-to-all-done.1 = f32[128,8,128]{2,1,0:T(8,128)S(1)} async-done(((f32[128,8,128]{2,1,0:T(8,128)}), f32[128,8,128]{2,1,0:T(8,128)S(1)}, u32[]{:S(2)}, u32[]{:S(2)}) %all-to-all-start.1) | async-done | bytes 524320 | tf_op jit(solution)/shard_map/all_to_all | solution.py:457
  71.0 0.0 collective-permute-start.1
  71.0 3.8 %collective-permute-start.4 = (f32[8,32,256]{2,1,0:T(8,128)S(1)}, f32[8,32,256]{2,1,0:T(8,128)S(1)}, u32[]{:S(2)}, u32[]{:S(2)}) collective-permute-start(f32[8,32,256]{2,1,0:T(8,128)S(1)} %get-tuple-element.14), channel_id=1, source_target_pairs={{24,32},{0,248},{25,33},{1,249},{26,34},{2,250},{27,35},{3,251},{2... | collective-permute-start | bytes 786440 | tf_op jit(solution)/shard_map/ppermute | solution.py:468
  74.9 0.0 collective-permute-done.5
  74.9 1.3 %collective-permute-start.6 = (f32[8,32,256]{2,1,0:T(8,128)S(1)}, f32[8,32,256]{2,1,0:T(8,128)S(1)}, u32[]{:S(2)}, u32[]{:S(2)}) collective-permute-start(f32[8,32,256]{2,1,0:T(8,128)S(1)} %collective-permute-done.5), channel_id=1, source_target_pairs={{16,32},{8,248},{17,33},{9,249},{18,34},{10,250},{19,35},{11,251},... | collective-permute-start | bytes 786440 | tf_op jit(solution)/shard_map/ppermute | solution.py:469
  76.2 0.0 copy-done.5
  76.2 0.1 fusion
  76.3 0.0 copy-done.3
  76.3 3.8 %shard_map.96.part1 = f32[8,4,32,256]{3,2,1,0:T(8,128)} custom-call(s32[8]{0:T(128)S(1)} %get-tuple-element.18.orient_ref, f32[3,24]{1,0:T(4,128)S(1)} %bitcast.13, f32[16,4,32,256]{3,2,1,0:T(8,128)} %phase_ref.5), custom_call_target="tpu_custom_call" | custom-call | flops 10000000 | bytes 10485760 | tf_op jit(solution)/shard_map/pallas_call | solution.py:503
  80.1 0.0 copy-start
  80.1 0.0 copy-start.2
  80.1 0.0 copy-start.4
  80.1 0.0 copy-start.6
  80.1 3.9 %shard_map.95.part0 = f32[8,4,32,256]{3,2,1,0:T(8,128)} custom-call(s32[8]{0:T(128)S(1)} %get-tuple-element.19.orient_ref, f32[3,24]{1,0:T(4,128)S(1)} %bitcast.14, f32[16,4,32,256]{3,2,1,0:T(8,128)} %phase_ref.5), custom_call_target="tpu_custom_call" | custom-call | flops 10000000 | bytes 10485760 | tf_op jit(solution)/shard_map/pallas_call | solution.py:503
  84.0 12.7 %collective-permute-done.4.far = f32[8,32,256]{2,1,0:T(8,128)S(1)} collective-permute-done((f32[8,32,256]{2,1,0:T(8,128)S(1)}, f32[8,32,256]{2,1,0:T(8,128)S(1)}, u32[]{:S(2)}, u32[]{:S(2)}) %collective-permute-start.4) | collective-permute-done | bytes 262176 | tf_op jit(solution)/shard_map/ppermute | solution.py:468
  96.7 2.6 %collective-permute-done.6.carried = f32[8,32,256]{2,1,0:T(8,128)S(1)} collective-permute-done((f32[8,32,256]{2,1,0:T(8,128)S(1)}, f32[8,32,256]{2,1,0:T(8,128)S(1)}, u32[]{:S(2)}, u32[]{:S(2)}) %collective-permute-start.6) | collective-permute-done | bytes 262176 | tf_op jit(solution)/shard_map/ppermute | solution.py:469
  99.3 0.0 collective-permute-done.2.near_low
  99.3 0.0 collective-permute-done.3.near_high
  99.3 1.7 %edges.1 = (f32[16,32,256]{2,1,0:T(8,128)}, f32[16,32,256]{2,1,0:T(8,128)}) custom-call(s32[3]{0:T(128)S(1)} %pad_add_fusion.place_ref, s32[16]{0:T(128)S(1)} %copy-done.5, f32[3,24]{1,0:T(4,128)S(1)} %bitcast.15, f32[16,32,256]{2,1,0:T(8,128)S(1)} %collective-permute-done.2.near_low, f32[16,32,256]{2,1,0:T(8,128)S(1)} %collective-permute-done.3.near_high, ...), custom_call_target="tpu_custom_call" | custom-call | flops 1000000 | bytes 3145728 | tf_op jit(solution)/shard_map/edges/pallas_call | solution.py:486
  100.9 0.0 collective-permute-done.1.other_ref
  100.9 0.0 copy-done
  100.9 0.0 copy-done.2
  101.0 0.0 copy-done.4
  101.0 0.0 copy-done.6
  101.0 6.0 %update.1 = (f32[16,4,32,256]{3,2,1,0:T(8,128)}, f32[6,4,32,256]{3,2,1,0:T(8,128)}) custom-call(s32[3]{0:T(128)S(1)} %pad_add_fusion.place_ref, s32[16]{0:T(128)S(1)} %copy-done.6, f32[6,12]{1,0:T(8,128)S(1)} %bitcast.17, f32[1024,128]{1,0:T(8,128)S(1)} %bitcast.11, f32[1024,128]{1,0:T(8,128)S(1)} %collective-permute-done.1.other_ref, ...), custom_call_target="tpu_custom_call" | custom-call | flops 100000000 | bytes 12582912 | tf_op jit(solution)/shard_map/update/pallas_call | solution.py:521
Async XLA Ops:
  0.7 41.5 %copy-start.1 = (bf16[896,512]{1,0:T(8,128)(2,1)S(1)}, bf16[896,512]{1,0:T(8,128)(2,1)}, u32[]{:S(2)}) copy-start(bf16[896,512]{1,0:T(8,128)(2,1)} %constant.50.clone.table) | copy-start | bytes 2752516
  4.9 2.0 %collective-permute-start = (f32[1024,128]{1,0:T(8,128)S(1)}, f32[1024,128]{1,0:T(8,128)S(1)}, u32[]{:S(2)}, u32[]{:S(2)}) collective-permute-start(f32[1024,128]{1,0:T(8,128)S(1)} %get-tuple-element.11), channel_id=1, source_target_pairs={{0,1},{1,0},{2,3},{3,2},{4,5},{5,4},{6,7},{7,6},{8,9},{9,8},{10,11... | collective-permute-start | bytes 1572872 | tf_op jit(solution)/shard_map/ppermute | solution.py:461
  7.0 69.2 %copy-start.5 = (s32[16]{0:T(128)S(1)}, s32[16]{0:T(128)}, u32[]{:S(2)}) copy-start(s32[16]{0:T(128)} %orient_ref.1) | copy-start | bytes 196
  7.0 69.3 %copy-start.3 = (f32[24,3]{0,1:T(4,128)S(1)}, f32[24,3]{0,1:T(4,128)}, u32[]{:S(2)}) copy-start(f32[24,3]{0,1:T(4,128)} %param.9) | copy-start | bytes 868
  45.2 25.9 %all-to-all-start.1 = ((f32[128,8,128]{2,1,0:T(8,128)}), f32[128,8,128]{2,1,0:T(8,128)S(1)}, u32[]{:S(2)}, u32[]{:S(2)}) async-start(f32[128,8,128]{2,1,0:T(8,128)} %bitcast.6), calls=%async_computation.1 | async-start | bytes 1048576 | tf_op jit(solution)/shard_map/all_to_all | solution.py:457
  51.8 23.1 %collective-permute-start.5 = (f32[8,32,256]{2,1,0:T(8,128)S(1)}, f32[8,32,256]{2,1,0:T(8,128)S(1)}, u32[]{:S(2)}, u32[]{:S(2)}) collective-permute-start(f32[8,32,256]{2,1,0:T(8,128)S(1)} %get-tuple-element.15), channel_id=1, source_target_pairs={{24,16},{0,8},{25,17},{1,9},{26,18},{2,10},{27,19},{3,11},{28,20},... | collective-permute-start | bytes 786440 | tf_op jit(solution)/shard_map/ppermute | solution.py:465
  55.2 44.1 %collective-permute-start.2 = (f32[16,32,256]{2,1,0:T(8,128)S(1)}, f32[16,32,256]{2,1,0:T(8,128)S(1)}, u32[]{:S(2)}, u32[]{:S(2)}) collective-permute-start(f32[16,32,256]{2,1,0:T(8,128)S(1)} %get-tuple-element.12), channel_id=1, source_target_pairs={{0,8},{8,16},{16,24},{1,9},{9,17},{17,25},{2,10},{10,18},{18,26},{... | collective-permute-start | bytes 1572872 | tf_op jit(solution)/shard_map/ppermute | solution.py:466
  56.5 42.8 %collective-permute-start.3 = (f32[16,32,256]{2,1,0:T(8,128)S(1)}, f32[16,32,256]{2,1,0:T(8,128)S(1)}, u32[]{:S(2)}, u32[]{:S(2)}) collective-permute-start(f32[16,32,256]{2,1,0:T(8,128)S(1)} %get-tuple-element.13), channel_id=1, source_target_pairs={{8,0},{16,8},{24,16},{9,1},{17,9},{25,17},{10,2},{18,10},{26,18},{... | collective-permute-start | bytes 1572872 | tf_op jit(solution)/shard_map/ppermute | solution.py:467
  71.0 29.9 %collective-permute-start.1 = (f32[1024,128]{1,0:T(8,128)S(1)}, f32[1024,128]{1,0:T(8,128)S(1)}, u32[]{:S(2)}, u32[]{:S(2)}) collective-permute-start(f32[1024,128]{1,0:T(8,128)S(1)} %bitcast.10), channel_id=1, source_target_pairs={{0,1},{1,0},{2,3},{3,2},{4,5},{5,4},{6,7},{7,6},{8,9},{9,8},{10,11... | collective-permute-start | bytes 1572872 | tf_op jit(solution)/shard_map/ppermute | solution.py:484
  71.0 25.6 %collective-permute-start.4 = (f32[8,32,256]{2,1,0:T(8,128)S(1)}, f32[8,32,256]{2,1,0:T(8,128)S(1)}, u32[]{:S(2)}, u32[]{:S(2)}) collective-permute-start(f32[8,32,256]{2,1,0:T(8,128)S(1)} %get-tuple-element.14), channel_id=1, source_target_pairs={{24,32},{0,248},{25,33},{1,249},{26,34},{2,250},{27,35},{3,251},{2... | collective-permute-start | bytes 786440 | tf_op jit(solution)/shard_map/ppermute | solution.py:468
  74.9 24.4 %collective-permute-start.6 = (f32[8,32,256]{2,1,0:T(8,128)S(1)}, f32[8,32,256]{2,1,0:T(8,128)S(1)}, u32[]{:S(2)}, u32[]{:S(2)}) collective-permute-start(f32[8,32,256]{2,1,0:T(8,128)S(1)} %collective-permute-done.5), channel_id=1, source_target_pairs={{16,32},{8,248},{17,33},{9,249},{18,34},{10,250},{19,35},{11,251},... | collective-permute-start | bytes 786440 | tf_op jit(solution)/shard_map/ppermute | solution.py:469
  80.1 20.9 %copy-start = (f32[16,4,32,256]{3,2,1,0:T(8,128)S(1)}, f32[16,4,32,256]{3,2,1,0:T(8,128)}, u32[]{:S(2)}) copy-start(f32[16,4,32,256]{3,2,1,0:T(8,128)} %phase_ref.5) | copy-start | bytes 6291460
  80.1 20.9 %copy-start.2 = (bf16[6,256,256]{2,1,0:T(8,128)(2,1)S(1)}, bf16[6,256,256]{2,1,0:T(8,128)(2,1)}, u32[]{:S(2)}) copy-start(bf16[6,256,256]{2,1,0:T(8,128)(2,1)} %constant.51.clone.table) | copy-start | bytes 2359300
  80.1 20.9 %copy-start.4 = (f32[12,6]{0,1:T(8,128)S(1)}, f32[12,6]{0,1:T(8,128)}, u32[]{:S(2)}) copy-start(f32[12,6]{0,1:T(8,128)} %param.10) | copy-start | bytes 868
  80.1 20.9 %copy-start.6 = (s32[16]{0:T(128)S(1)}, s32[16]{0:T(128)}, u32[]{:S(2)}) copy-start(s32[16]{0:T(128)} %family_ref.1) | copy-start | bytes 196

commit v3 on v2

--- a/solution.py
+++ b/solution.py
@@ -1,3 +1,5 @@
+import functools
+
 import jax
 import jax.numpy as jnp
 import numpy as np
@@ -215,7 +217,7 @@
 
 def spectral_kernel(place_ref, in_ref, table, out_ref):
     half, kz = place_ref[0], place_ref[1]
-    rows = ((in_ref[:, 0] + in_ref[:, 1]) + (in_ref[:, 2] + in_ref[:, 3])).reshape(256, 128)
+    rows = ((in_ref[0] + in_ref[1]) + (in_ref[2] + in_ref[3])).reshape(256, 128)
     lane1 = lax.broadcasted_iota(jnp.int32, (1, 128), 1)
     sign = jnp.where(lane1 < 64, 1.0, -1.0).astype(F32)
 
@@ -277,30 +279,35 @@
     answer = dot3((table[384:640, :384], table[640:896, :384]), split(stacked))
     kind = lax.broadcasted_iota(jnp.int32, (256, 128), 0) % 8
     answer = jnp.where(kind == 6, rows, answer).reshape(32, 8, 128)
-    for copy in range(out_ref.shape[1]):
-        out_ref[:, copy] = answer
-
-
-def local_kernel(orient_ref, kappa_ref, phase_ref, part_ref):
-    step = pl.program_id(0)
-    per_step = phase_ref.shape[0]
-    for index in range(per_step):
-        orient = orient_ref[step * per_step + index]
+    for copy in range(out_ref.shape[0]):
+        out_ref[copy] = answer
+
+
+def local_kernel(orient_low, orient_high, kappa_ref, phase_ref, part_ref):
+    half = orient_low.shape[0]
+
+    def one(place, carry, orient_ref, at):
+        orient = orient_ref[place]
+        variant = place + at
         kappa = [TIME_STEP * kappa_ref[d, orient] for d in range(3)]
         center = 1.0 - 2.0 * (kappa[0] + kappa[1] + kappa[2])
         for x in range(SLAB):
-            p = phase_ref[index, x]
+            p = phase_ref[variant, x]
             if x == 0:
-                beside = phase_ref[index, x + 1]
+                beside = phase_ref[variant, x + 1]
             elif x == SLAB - 1:
-                beside = phase_ref[index, x - 1]
+                beside = phase_ref[variant, x - 1]
             else:
-                beside = phase_ref[index, x - 1] + phase_ref[index, x + 1]
+                beside = phase_ref[variant, x - 1] + phase_ref[variant, x + 1]
             moved = kappa[0] * beside
             moved = moved + kappa[1] * (pltpu.roll(p, 1, 0) + pltpu.roll(p, NY - 1, 0))
             moved = moved + kappa[2] * (pltpu.roll(p, 1, 1) + pltpu.roll(p, NZ - 1, 1))
             cubic = (6.0 * TIME_STEP) - (TIME_STEP * (4.0 - 2.0 * CROSS_COUPLING)) * p
-            part_ref[index, x] = p * (center + p * cubic) + moved
+            part_ref[variant, x] = p * (center + p * cubic) + moved
+        return carry
+
+    lax.fori_loop(0, half, functools.partial(one, orient_ref=orient_low, at=0), 0)
+    lax.fori_loop(0, half, functools.partial(one, orient_ref=orient_high, at=half), 0)
 
 
 def edges_kernel(place_ref, orient_ref, kappa_ref, near_low, near_high, far, carried, low_out, high_out):
@@ -314,7 +321,7 @@
 
 
 def update_kernel(
-    place_ref, family_ref, eps_ref, mine_ref, other_ref, table, phase_ref, low_hbm, high_hbm, part0, part1,
+    place_ref, family_ref, eps_ref, mine_ref, other_ref, table, phase_ref, low_hbm, high_hbm, part_hbm,
     next_ref, stress_ref, base, low_ref, high_ref, part_ref, sems,
 ):
     step = pl.program_id(0)
@@ -323,9 +330,8 @@
     count = phase_ref.shape[0] // per_step
 
     def part_start(index):
-        source, at = (part0, index) if index < count // 2 else (part1, index - count // 2)
-        rows, target = pl.ds(at * per_step, per_step), pl.ds(index * per_step, per_step)
-        return pltpu.make_async_copy(source.at[rows], part_ref.at[target], sems.at[index])
+        rows = pl.ds(index * per_step, per_step)
+        return pltpu.make_async_copy(part_hbm.at[rows], part_ref.at[rows], sems.at[index])
 
     edge_copies = [
         pltpu.make_async_copy(low_hbm, low_ref, sems.at[count]),
@@ -361,7 +367,7 @@
             copy.wait()
 
     rows = pl.ds(step * per_step, per_step)
-    pltpu.make_async_copy(part0.at[pl.ds(0, per_step)], part_ref.at[rows], sems.at[step]).wait()
+    pltpu.make_async_copy(part_hbm.at[pl.ds(0, per_step)], part_ref.at[rows], sems.at[step]).wait()
     for index in range(per_step):
         variant = step * per_step + index
         family = family_ref[variant]
@@ -421,7 +427,7 @@
     variants = phase_field.shape[0]
     place = lax.axis_index("vert")
     core = (place % 2).astype(jnp.int32)
-    kz_own = (lax.axis_index("gx") * runs + place // 2).astype(jnp.int32)
+    kz_own = (place // 2 * slabs + lax.axis_index("gx")).astype(jnp.int32)
     place_arr = jnp.stack([core, kz_own, (lax.axis_index("gx") % SLAB).astype(jnp.int32)])
     eps_t, kappa_t = eps_table.T, kappa_table.T
 
@@ -429,7 +435,7 @@
     ry, rp = y_tables()
     hbm = pl.BlockSpec(memory_space=pltpu.HBM)
 
-    planes = [jax.ShapeDtypeStruct((count, NY, NZ), F32) for count in (variants, variants // 2)]
+    planes = [pltpu.HBM((count, NY, NZ), F32) for count in (variants, variants // 2)]
     spread = jax.ShapeDtypeStruct((1024, 128), F32)
     keep, send, last, front, far, relay = pl.pallas_call(
         sums_kernel,
@@ -451,7 +457,7 @@
     )(place_arr, *(in_hbm(value) for value in (family_index, eps_t, phase_field, stacked_halves(tz, ry, rp))))
 
     partner = [(i, i ^ 1) for i in range(groups)]
-    same_core = [[g * groups + 2 * r + c for g in range(slabs) for r in range(runs)] for c in range(2)]
+    same_core = [[g * groups + 2 * r + c for r in range(runs) for g in range(slabs)] for c in range(2)]
 
     def exchange(value):
         return lax.all_to_all(
@@ -468,13 +474,13 @@
     far = lax.ppermute(far, both, across)
     carry = lax.ppermute(relay, both, carried)
 
-    arrived = exchange(summed.reshape(128, 8, 128)).reshape(slabs, runs, 8, 128)
+    arrived = exchange(summed.reshape(128, 8, 128)).reshape(runs, slabs, 8, 128)
 
     answers = pl.pallas_call(
         spectral_kernel,
         in_specs=[smem()] + [vmem()] * 2,
         out_specs=vmem(),
-        out_shape=jax.ShapeDtypeStruct((slabs, runs, 8, 128), F32),
+        out_shape=jax.ShapeDtypeStruct((runs, slabs, 8, 128), F32),
         compiler_params=limit(12),
         cost_estimate=pl.CostEstimate(flops=10**8, bytes_accessed=4 << 20, transcendentals=0),
         name="spectral",
@@ -493,35 +499,23 @@
         name="edges",
     )(place_arr, orient_index, kappa_t, near_low, near_high, far, carry)
 
+    orients = [orient_index[: variants // 2], orient_index[variants // 2 :]]
+    part = pl.pallas_call(
+        local_kernel,
+        in_specs=[smem()] * 3 + [vmem()],
+        out_specs=vmem(),
+        out_shape=pltpu.HBM(phase_field.shape, F32),
+        compiler_params=limit(8),
+        cost_estimate=pl.CostEstimate(flops=10**7, bytes_accessed=10 << 20, transcendentals=0),
+        name="local",
+    )(*orients, kappa_t, phase_field)
+
     per_step = 2
     whole = pl.BlockSpec((per_step, SLAB, NY, NZ), lambda i: (i, 0, 0, 0))
-    half = variants // 2
-    orients = [orient_index[:half], orient_index[half:]]
-    part = []
-    for index in range(2):
-        part.append(
-            pl.pallas_call(
-                local_kernel,
-                grid=(half // per_step,),
-                in_specs=[
-                    smem(),
-                    smem(),
-                    pl.BlockSpec(whole.block_shape, lambda i, at=index * half // per_step: (i + at, 0, 0, 0)),
-                ],
-                out_specs=whole,
-                out_shape=pltpu.HBM((half, SLAB, NY, NZ), F32),
-                compiler_params=limit(4),
-                cost_estimate=pl.CostEstimate(flops=10**7, bytes_accessed=10 << 20, transcendentals=0),
-            )(
-                orients[index], kappa_t,
-                in_hbm(phase_field),
-            )
-        )
-
     phase_next, stress = pl.pallas_call(
         update_kernel,
         grid=(variants // per_step,),
-        in_specs=[smem()] * 3 + [vmem()] * 4 + [hbm] * 4,
+        in_specs=[smem()] * 3 + [vmem()] * 4 + [hbm] * 3,
         out_specs=[whole, pl.BlockSpec((COMPS, SLAB, NY, NZ), lambda i: (0, 0, 0, 0))],
         out_shape=[
             jax.ShapeDtypeStruct(phase_field.shape, F32),
@@ -540,7 +534,7 @@
     )(
         place_arr, family_index, eps_t, mine, other,
         stacked_halves(np.linalg.inv(ry), np.linalg.inv(rp), np.linalg.inv(tz).T),
-        phase_field, *(in_hbm(value) for value in (edge_low, edge_high, *part)),
+        phase_field, *(in_hbm(value) for value in (edge_low, edge_high, part)),
     )
     return phase_next, stress
 

time: 108 us -> 109 us (level)
  Pallas kernels: 22.5 us -> 19.3 us
  starting transfers between devices: 17.8 us -> 20 us
  waiting for transfers between devices: 30.4 us -> 32.5 us
    pallas_call x2 -> x1, Pallas kernels: 7.73 us -> 4.21 us  [step(): pl.pallas_call(local_kernel, in_specs=[smem()] * 3 + [vmem()], out_specs=...]
    ppermute x1, waiting for transfers between devices: 2.57 us -> 5.58 us  [step(): carry = lax.ppermute(relay, both, carried)]
    ppermute x1, starting transfers between devices: 3.83 us -> 5.14 us  [step(): far = lax.ppermute(far, both, across)]
    all_to_all x1, waiting for transfers between devices: 13.2 us -> 12 us  [exchange(): lax.all_to_all(value, ('gx', 'vert'), split_axis=0, concat_axis=0, axis_i...]
  transfers between devices with their start and end apart: 8 -> 8, of which waited for: 4 -> 4; matrix products, arithmetic and copies ran while one was open for 0% -> 0% of each run, Pallas kernels for 9% -> 6%
where the time goes in v3:
time: 109 us; the launch traced here: 108 us
  blocking collectives  34.7 us (32%)
  waiting for transfers between devices  32.5 us (30%)
  starting transfers between devices  20 us (18%)
  Pallas kernels  19.3 us (18%)
    all_to_all x1, blocking collectives, exchange(): lax.all_to_all(value, ('gx', 'vert'), split_axis=0, concat_axis=0, axis_i...  34.7 us
    ppermute x1, waiting for transfers between devices, step(): far = lax.ppermute(far, both, across)  13 us
    all_to_all x1, waiting for transfers between devices, exchange(): lax.all_to_all(value, ('gx', 'vert'), split_axis=0, concat_axis=0, axis_i...  12 us
    all_to_all x1, starting transfers between devices, exchange(): lax.all_to_all(value, ('gx', 'vert'), split_axis=0, concat_axis=0, axis_i...  6.78 us
    pallas_call x1, Pallas kernels, step(): pl.pallas_call(update_kernel, grid=(variants // per_step,), in_specs=[sme...  5.89 us
    ppermute x1, waiting for transfers between devices, step(): carry = lax.ppermute(relay, both, carried)  5.58 us
    ppermute x1, starting transfers between devices, step(): far = lax.ppermute(far, both, across)  5.14 us
    pallas_call x1, Pallas kernels, step(): pl.pallas_call(local_kernel, in_specs=[smem()] * 3 + [vmem()], out_specs=...  4.21 us
  transfers between devices with their start and end apart: 8, of which 4 were waited for; matrix products, arithmetic and copies ran while one was open for 0% of the time, Pallas kernels for 6%

profile of v3, /device:TPU:32, one launch (start us, length us, event | category | flops | bytes accessed | tf_op | source)
XLA Modules:
  0.0 107.6 jit_solution(16287477067550133543)
XLA Ops:
  0.7 0.1 pad_add_fusion.place_ref
  0.7 0.0 copy-start.1
  0.7 4.2 %sums.1 = (f32[1024,128]{1,0:T(8,128)S(1)}, f32[1024,128]{1,0:T(8,128)S(1)}, f32[16,32,256]{2,1,0:T(8,128)}, f32[16,32,256]{2,1,0:T(8,128)}, f32[8,32,256]{2,1,0:T(8,128)}, /*index=5*/f32[8,32,256]{2,1,0:T(8,128)}) custom-call(s32[3]{0:T(128)S(1)} %pad_add_fusion.place_ref, s32[16]{0:T(128)} %family_ref.1, f32[6,12]{1,0:T(8,128)} %bitcast.13, ...), custom_call_target="tpu_custom_call" | custom-call | flops 100000000 | bytes 9437184 | tf_op jit(solution)/shard_map/sums/pallas_call | solution.py:440
  4.9 0.1 collective-permute-start
  5.0 1.9 %collective-permute-done = f32[1024,128]{1,0:T(8,128)S(1)} collective-permute-done((f32[1024,128]{1,0:T(8,128)S(1)}, f32[1024,128]{1,0:T(8,128)S(1)}, u32[]{:S(2)}, u32[]{:S(2)}) %collective-permute-start) | collective-permute-done | bytes 524320 | tf_op jit(solution)/shard_map/ppermute | solution.py:467
  6.9 0.1 add_bitcast_fusion
  7.0 0.0 copy-start.7
  7.0 0.0 copy-start.5
  7.0 0.0 copy-start
  7.0 0.0 copy-start.4
  7.0 34.7 %all_to_all.10 = f32[128,8,128]{2,1,0:T(8,128)S(1)} all-to-all(f32[128,8,128]{2,1,0:T(8,128)S(1)} %add_bitcast_fusion), channel_id=1, replica_groups={{0,8,16,24,32,40,48,56,64,72,80,88,96,104,112,120,128,136,144,152,160,1..., dimensions={0} | all-to-all | bytes 1048576 | tf_op jit(solution)/shard_map/all_to_all | solution.py:463
  41.8 0.0 copy-done.1
  41.8 3.0 %spectral.1 = f32[4,32,8,128]{3,2,1,0:T(8,128)} custom-call(s32[3]{0:T(128)S(1)} %pad_add_fusion.place_ref, f32[4,32,8,128]{3,2,1,0:T(8,128)S(1)} %bitcast.12, bf16[896,512]{1,0:T(8,128)(2,1)S(1)} %copy-done.1), custom_call_target="tpu_custom_call" | custom-call | flops 100000000 | bytes 4194304 | tf_op jit(solution)/shard_map/spectral/pallas_call | solution.py:479
  44.7 6.8 %all-to-all-start.1 = ((f32[128,8,128]{2,1,0:T(8,128)}), f32[128,8,128]{2,1,0:T(8,128)S(1)}, u32[]{:S(2)}, u32[]{:S(2)}) async-start(f32[128,8,128]{2,1,0:T(8,128)} %bitcast.6), calls=%async_computation.1 | async-start | bytes 1048576 | tf_op jit(solution)/shard_map/all_to_all | solution.py:463
  51.5 4.1 %collective-permute-start.5 = (f32[8,32,256]{2,1,0:T(8,128)}, f32[8,32,256]{2,1,0:T(8,128)}, u32[]{:S(2)}, u32[]{:S(2)}) collective-permute-start(f32[8,32,256]{2,1,0:T(8,128)} %get-tuple-element.15), channel_id=1, source_target_pairs={{24,16},{0,8},{25,17},{1,9},{26,18},{2,10},{27,19},{3,11},{28,20},... | collective-permute-start | bytes 786440 | tf_op jit(solution)/shard_map/ppermute | solution.py:471
  55.6 1.3 %collective-permute-start.2 = (f32[16,32,256]{2,1,0:T(8,128)}, f32[16,32,256]{2,1,0:T(8,128)S(1)}, u32[]{:S(2)}, u32[]{:S(2)}) collective-permute-start(f32[16,32,256]{2,1,0:T(8,128)} %get-tuple-element.12), channel_id=1, source_target_pairs={{0,8},{8,16},{16,24},{1,9},{9,17},{17,25},{2,10},{10,18},{18,26},{... | collective-permute-start | bytes 1572872 | tf_op jit(solution)/shard_map/ppermute | solution.py:472
  56.9 1.3 %collective-permute-start.3 = (f32[16,32,256]{2,1,0:T(8,128)}, f32[16,32,256]{2,1,0:T(8,128)}, u32[]{:S(2)}, u32[]{:S(2)}) collective-permute-start(f32[16,32,256]{2,1,0:T(8,128)} %get-tuple-element.13), channel_id=1, source_target_pairs={{8,0},{16,8},{24,16},{9,1},{17,9},{25,17},{10,2},{18,10},{26,18},{... | collective-permute-start | bytes 1572872 | tf_op jit(solution)/shard_map/ppermute | solution.py:473
  58.2 12.0 %all-to-all-done.1 = f32[128,8,128]{2,1,0:T(8,128)S(1)} async-done(((f32[128,8,128]{2,1,0:T(8,128)}), f32[128,8,128]{2,1,0:T(8,128)S(1)}, u32[]{:S(2)}, u32[]{:S(2)}) %all-to-all-start.1) | async-done | bytes 524320 | tf_op jit(solution)/shard_map/all_to_all | solution.py:463
  70.2 0.0 collective-permute-start.1
  70.2 0.0 copy-done.7
  70.2 5.1 %collective-permute-start.4 = (f32[8,32,256]{2,1,0:T(8,128)S(1)}, f32[8,32,256]{2,1,0:T(8,128)S(1)}, u32[]{:S(2)}, u32[]{:S(2)}) collective-permute-start(f32[8,32,256]{2,1,0:T(8,128)S(1)} %copy-done.7), channel_id=1, source_target_pairs={{24,32},{0,248},{25,33},{1,249},{26,34},{2,250},{27,35},{3,251},{2... | collective-permute-start | bytes 786440 | tf_op jit(solution)/shard_map/ppermute | solution.py:474
  75.4 0.0 collective-permute-done.5
  75.4 1.3 %collective-permute-start.6 = (f32[8,32,256]{2,1,0:T(8,128)}, f32[8,32,256]{2,1,0:T(8,128)S(1)}, u32[]{:S(2)}, u32[]{:S(2)}) collective-permute-start(f32[8,32,256]{2,1,0:T(8,128)} %collective-permute-done.5), channel_id=1, source_target_pairs={{16,32},{8,248},{17,33},{9,249},{18,34},{10,250},{19,35},{11,251},... | collective-permute-start | bytes 786440 | tf_op jit(solution)/shard_map/ppermute | solution.py:475
  76.7 0.0 copy-done.5
  76.7 0.1 fusion
  76.8 0.0 copy-done
  76.8 0.0 copy-done.4
  76.8 0.0 copy-start.2
  76.8 0.0 copy-start.3
  76.8 0.0 copy-start.6
  76.8 4.2 %local.1.part_hbm = f32[16,4,32,256]{3,2,1,0:T(8,128)} custom-call(s32[8]{0:T(128)S(1)} %get-tuple-element.19.orient_low, s32[8]{0:T(128)S(1)} %get-tuple-element.18.orient_high, f32[3,24]{1,0:T(4,128)S(1)} %bitcast.15, f32[16,4,32,256]{3,2,1,0:T(8,128)S(1)} %copy-done), custom_call_target="tpu_custom_call" | custom-call | flops 10000000 | bytes 10485760 | tf_op jit(solution)/shard_map/local/pallas_call | solution.py:503
  81.0 13.0 %collective-permute-done.4.far = f32[8,32,256]{2,1,0:T(8,128)S(1)} collective-permute-done((f32[8,32,256]{2,1,0:T(8,128)S(1)}, f32[8,32,256]{2,1,0:T(8,128)S(1)}, u32[]{:S(2)}, u32[]{:S(2)}) %collective-permute-start.4) | collective-permute-done | bytes 262176 | tf_op jit(solution)/shard_map/ppermute | solution.py:474
  94.0 5.6 %collective-permute-done.6.carried = f32[8,32,256]{2,1,0:T(8,128)S(1)} collective-permute-done((f32[8,32,256]{2,1,0:T(8,128)}, f32[8,32,256]{2,1,0:T(8,128)S(1)}, u32[]{:S(2)}, u32[]{:S(2)}) %collective-permute-start.6) | collective-permute-done | bytes 262176 | tf_op jit(solution)/shard_map/ppermute | solution.py:475
  99.6 0.0 collective-permute-done.2.near_low
  99.6 0.0 collective-permute-done.3.near_high
  99.6 2.1 %edges.1 = (f32[16,32,256]{2,1,0:T(8,128)}, f32[16,32,256]{2,1,0:T(8,128)}) custom-call(s32[3]{0:T(128)S(1)} %pad_add_fusion.place_ref, s32[16]{0:T(128)S(1)} %copy-done.5, f32[3,24]{1,0:T(4,128)S(1)} %bitcast.16, f32[16,32,256]{2,1,0:T(8,128)S(1)} %collective-permute-done.2.near_low, f32[16,32,256]{2,1,0:T(8,128)} %collective-permute-done.3.near_high, ...), custom_call_target="tpu_custom_call" | custom-call | flops 1000000 | bytes 3145728 | tf_op jit(solution)/shard_map/edges/pallas_call | solution.py:492
  101.7 0.0 collective-permute-done.1.other_ref
  101.7 0.0 copy-done.2
  101.7 0.0 copy-done.3
  101.7 0.0 copy-done.6
  101.7 5.9 %update.1 = (f32[16,4,32,256]{3,2,1,0:T(8,128)}, f32[6,4,32,256]{3,2,1,0:T(8,128)}) custom-call(s32[3]{0:T(128)S(1)} %pad_add_fusion.place_ref, s32[16]{0:T(128)S(1)} %copy-done.6, f32[6,12]{1,0:T(8,128)S(1)} %bitcast.14, f32[1024,128]{1,0:T(8,128)S(1)} %bitcast.11, f32[1024,128]{1,0:T(8,128)S(1)} %collective-permute-done.1.other_ref, ...), custom_call_target="tpu_custom_call" | custom-call | flops 100000000 | bytes 12582912 | tf_op jit(solution)/shard_map/update/pallas_call | solution.py:515
Async XLA Ops:
  0.7 41.0 %copy-start.1 = (bf16[896,512]{1,0:T(8,128)(2,1)S(1)}, bf16[896,512]{1,0:T(8,128)(2,1)}, u32[]{:S(2)}) copy-start(bf16[896,512]{1,0:T(8,128)(2,1)} %constant.52.clone.table) | copy-start | bytes 2752516
  4.9 2.0 %collective-permute-start = (f32[1024,128]{1,0:T(8,128)S(1)}, f32[1024,128]{1,0:T(8,128)S(1)}, u32[]{:S(2)}, u32[]{:S(2)}) collective-permute-start(f32[1024,128]{1,0:T(8,128)S(1)} %get-tuple-element.11), channel_id=1, source_target_pairs={{0,1},{1,0},{2,3},{3,2},{4,5},{5,4},{6,7},{7,6},{8,9},{9,8},{10,11... | collective-permute-start | bytes 1572872 | tf_op jit(solution)/shard_map/ppermute | solution.py:467
  7.0 63.2 %copy-start.7 = (f32[8,32,256]{2,1,0:T(8,128)S(1)}, f32[8,32,256]{2,1,0:T(8,128)}, u32[]{:S(2)}) copy-start(f32[8,32,256]{2,1,0:T(8,128)} %get-tuple-element.14) | copy-start | bytes 786436
  7.0 69.7 %copy-start.5 = (s32[16]{0:T(128)S(1)}, s32[16]{0:T(128)}, u32[]{:S(2)}) copy-start(s32[16]{0:T(128)} %orient_ref.1) | copy-start | bytes 196
  7.0 69.8 %copy-start = (f32[16,4,32,256]{3,2,1,0:T(8,128)S(1)}, f32[16,4,32,256]{3,2,1,0:T(8,128)}, u32[]{:S(2)}) copy-start(f32[16,4,32,256]{3,2,1,0:T(8,128)} %phase_ref.3) | copy-start | bytes 6291460
  7.0 69.8 %copy-start.4 = (f32[24,3]{0,1:T(4,128)S(1)}, f32[24,3]{0,1:T(4,128)}, u32[]{:S(2)}) copy-start(f32[24,3]{0,1:T(4,128)} %param.9) | copy-start | bytes 868
  44.7 25.5 %all-to-all-start.1 = ((f32[128,8,128]{2,1,0:T(8,128)}), f32[128,8,128]{2,1,0:T(8,128)S(1)}, u32[]{:S(2)}, u32[]{:S(2)}) async-start(f32[128,8,128]{2,1,0:T(8,128)} %bitcast.6), calls=%async_computation.1 | async-start | bytes 1048576 | tf_op jit(solution)/shard_map/all_to_all | solution.py:463
  51.5 23.9 %collective-permute-start.5 = (f32[8,32,256]{2,1,0:T(8,128)}, f32[8,32,256]{2,1,0:T(8,128)}, u32[]{:S(2)}, u32[]{:S(2)}) collective-permute-start(f32[8,32,256]{2,1,0:T(8,128)} %get-tuple-element.15), channel_id=1, source_target_pairs={{24,16},{0,8},{25,17},{1,9},{26,18},{2,10},{27,19},{3,11},{28,20},... | collective-permute-start | bytes 786440 | tf_op jit(solution)/shard_map/ppermute | solution.py:471
  55.6 44.0 %collective-permute-start.2 = (f32[16,32,256]{2,1,0:T(8,128)}, f32[16,32,256]{2,1,0:T(8,128)S(1)}, u32[]{:S(2)}, u32[]{:S(2)}) collective-permute-start(f32[16,32,256]{2,1,0:T(8,128)} %get-tuple-element.12), channel_id=1, source_target_pairs={{0,8},{8,16},{16,24},{1,9},{9,17},{17,25},{2,10},{10,18},{18,26},{... | collective-permute-start | bytes 1572872 | tf_op jit(solution)/shard_map/ppermute | solution.py:472
  56.9 42.6 %collective-permute-start.3 = (f32[16,32,256]{2,1,0:T(8,128)}, f32[16,32,256]{2,1,0:T(8,128)}, u32[]{:S(2)}, u32[]{:S(2)}) collective-permute-start(f32[16,32,256]{2,1,0:T(8,128)} %get-tuple-element.13), channel_id=1, source_target_pairs={{8,0},{16,8},{24,16},{9,1},{17,9},{25,17},{10,2},{18,10},{26,18},{... | collective-permute-start | bytes 1572872 | tf_op jit(solution)/shard_map/ppermute | solution.py:473
  70.2 31.5 %collective-permute-start.1 = (f32[1024,128]{1,0:T(8,128)S(1)}, f32[1024,128]{1,0:T(8,128)S(1)}, u32[]{:S(2)}, u32[]{:S(2)}) collective-permute-start(f32[1024,128]{1,0:T(8,128)S(1)} %bitcast.10), channel_id=1, source_target_pairs={{0,1},{1,0},{2,3},{3,2},{4,5},{5,4},{6,7},{7,6},{8,9},{9,8},{10,11... | collective-permute-start | bytes 1572872 | tf_op jit(solution)/shard_map/ppermute | solution.py:490
  70.2 23.8 %collective-permute-start.4 = (f32[8,32,256]{2,1,0:T(8,128)S(1)}, f32[8,32,256]{2,1,0:T(8,128)S(1)}, u32[]{:S(2)}, u32[]{:S(2)}) collective-permute-start(f32[8,32,256]{2,1,0:T(8,128)S(1)} %copy-done.7), channel_id=1, source_target_pairs={{24,32},{0,248},{25,33},{1,249},{26,34},{2,250},{27,35},{3,251},{2... | collective-permute-start | bytes 786440 | tf_op jit(solution)/shard_map/ppermute | solution.py:474
  75.4 24.2 %collective-permute-start.6 = (f32[8,32,256]{2,1,0:T(8,128)}, f32[8,32,256]{2,1,0:T(8,128)S(1)}, u32[]{:S(2)}, u32[]{:S(2)}) collective-permute-start(f32[8,32,256]{2,1,0:T(8,128)} %collective-permute-done.5), channel_id=1, source_target_pairs={{16,32},{8,248},{17,33},{9,249},{18,34},{10,250},{19,35},{11,251},... | collective-permute-start | bytes 786440 | tf_op jit(solution)/shard_map/ppermute | solution.py:475
  76.8 24.9 %copy-start.2 = (bf16[6,256,256]{2,1,0:T(8,128)(2,1)S(1)}, bf16[6,256,256]{2,1,0:T(8,128)(2,1)}, u32[]{:S(2)}) copy-start(bf16[6,256,256]{2,1,0:T(8,128)(2,1)} %constant.53.clone.table) | copy-start | bytes 2359300
  76.8 24.9 %copy-start.3 = (f32[12,6]{0,1:T(8,128)S(1)}, f32[12,6]{0,1:T(8,128)}, u32[]{:S(2)}) copy-start(f32[12,6]{0,1:T(8,128)} %param.10) | copy-start | bytes 868
  76.8 24.9 %copy-start.6 = (s32[16]{0:T(128)S(1)}, s32[16]{0:T(128)}, u32[]{:S(2)}) copy-start(s32[16]{0:T(128)} %family_ref.1) | copy-start | bytes 196

commit v4 on v3

--- a/solution.py
+++ b/solution.py
@@ -22,6 +22,8 @@
 SLABS = 32
 HALF = NZ // 2
 COMPS = 6
+MEMBERS = [(0, 0), (8, 0), (16, 0), (24, 0), (1, 0), (9, 0), (17, 0), (25, 0), (2, 0), (10, 0), (18, 0), (26, 0), (3, 0), (11, 0), (19, 0), (27, 0), (4, 0), (12, 0), (20, 0), (28, 0), (5, 0), (13, 0), (21, 0), (29, 0), (6, 0), (14, 0), (22, 0), (30, 0), (7, 0), (15, 0), (23, 0), (31, 0), (0, 1), (8, 1), (16, 1), (24, 1), (1, 1), (9, 1), (17, 1), (25, 1), (2, 1), (10, 1), (18, 1), (26, 1), (3, 1), (11, 1), (19, 1), (27, 1), (4, 1), (12, 1), (20, 1), (28, 1), (5, 1), (13, 1), (21, 1), (29, 1), (6, 1), (14, 1), (22, 1), (30, 1), (7, 1), (15, 1), (23, 1), (31, 1), (0, 2), (8, 2), (16, 2), (24, 2), (1, 2), (9, 2), (17, 2), (25, 2), (2, 2), (10, 2), (18, 2), (26, 2), (3, 2), (11, 2), (19, 2), (27, 2), (4, 2), (12, 2), (20, 2), (28, 2), (5, 2), (13, 2), (21, 2), (29, 2), (6, 2), (14, 2), (22, 2), (30, 2), (7, 2), (15, 2), (23, 2), (31, 2), (0, 3), (8, 3), (16, 3), (24, 3), (1, 3), (9, 3), (17, 3), (25, 3), (2, 3), (10, 3), (18, 3), (26, 3), (3, 3), (11, 3), (19, 3), (27, 3), (4, 3), (12, 3), (20, 3), (28, 3), (5, 3), (13, 3), (21, 3), (29, 3), (6, 3), (14, 3), (22, 3), (30, 3), (7, 3), (15, 3), (23, 3), (31, 3)]
+ROW_SLABS = [0, 8, 16, 24, 1, 9, 17, 25, 2, 10, 18, 26, 3, 11, 19, 27, 4, 12, 20, 28, 5, 13, 21, 29, 6, 14, 22, 30, 7, 15, 23, 31]
 
 
 def z_table():
@@ -74,6 +76,7 @@
                 right[1, plane_in, low, 0, plane_out, low] = np.round(np.sin(theta))
                 right[0, plane_in, low, 1, plane_out, low] = -np.round(np.sin(theta))
                 right[1, plane_in, low, 1, plane_out, low] = np.round(np.cos(theta))
+    left, back = left[..., ROW_SLABS, :], back[ROW_SLABS]
     right = right.reshape(128, 128)
     return left.reshape(192, 512), back.reshape(256, 384), np.cos(turn), np.sin(turn), right, right.T.copy()
 
@@ -217,7 +220,7 @@
 
 def spectral_kernel(place_ref, in_ref, table, out_ref):
     half, kz = place_ref[0], place_ref[1]
-    rows = ((in_ref[0] + in_ref[1]) + (in_ref[2] + in_ref[3])).reshape(256, 128)
+    rows = ((in_ref[:, 0] + in_ref[:, 1]) + (in_ref[:, 2] + in_ref[:, 3])).reshape(256, 128)
     lane1 = lax.broadcasted_iota(jnp.int32, (1, 128), 1)
     sign = jnp.where(lane1 < 64, 1.0, -1.0).astype(F32)
 
@@ -278,9 +281,9 @@
     stacked = jnp.concatenate([value, turned(value)], axis=0)
     answer = dot3((table[384:640, :384], table[640:896, :384]), split(stacked))
     kind = lax.broadcasted_iota(jnp.int32, (256, 128), 0) % 8
-    answer = jnp.where(kind == 6, rows, answer).reshape(32, 8, 128)
-    for copy in range(out_ref.shape[0]):
-        out_ref[copy] = answer
+    answer = jnp.where(kind == 6, rows, answer).reshape(out_ref.shape[0], out_ref.shape[2], 8, 128)
+    for copy in range(out_ref.shape[1]):
+        out_ref[:, copy] = answer
 
 
 def local_kernel(orient_low, orient_high, kappa_ref, phase_ref, part_ref):
@@ -421,13 +424,15 @@
 
 
 def step(phase_field, kappa_table, eps_table, orient_index, family_index):
-    slabs = lax.axis_size("gx")
     groups = lax.axis_size("vert")
     runs = groups // 2
     variants = phase_field.shape[0]
     place = lax.axis_index("vert")
     core = (place % 2).astype(jnp.int32)
-    kz_own = (place // 2 * slabs + lax.axis_index("gx")).astype(jnp.int32)
+    slab = lax.axis_index("gx")
+    kz_own = (
+        place // 2 * 32 + slab // 8 * 1 + slab // 4 % 2 * 16 + slab % 4 * 4
+    ).astype(jnp.int32)
     place_arr = jnp.stack([core, kz_own, (lax.axis_index("gx") % SLAB).astype(jnp.int32)])
     eps_t, kappa_t = eps_table.T, kappa_table.T
 
@@ -457,7 +462,7 @@
     )(place_arr, *(in_hbm(value) for value in (family_index, eps_t, phase_field, stacked_halves(tz, ry, rp))))
 
     partner = [(i, i ^ 1) for i in range(groups)]
-    same_core = [[g * groups + 2 * r + c for r in range(runs) for g in range(slabs)] for c in range(2)]
+    same_core = [[g * groups + 2 * r + c for g, r in MEMBERS] for c in range(2)]
 
     def exchange(value):
         return lax.all_to_all(
@@ -474,13 +479,13 @@
     far = lax.ppermute(far, both, across)
     carry = lax.ppermute(relay, both, carried)
 
-    arrived = exchange(summed.reshape(128, 8, 128)).reshape(runs, slabs, 8, 128)
+    arrived = exchange(summed.reshape(128, 8, 128)).reshape(1, runs, 32, 8, 128)
 
     answers = pl.pallas_call(
         spectral_kernel,
         in_specs=[smem()] + [vmem()] * 2,
         out_specs=vmem(),
-        out_shape=jax.ShapeDtypeStruct((runs, slabs, 8, 128), F32),
+        out_shape=jax.ShapeDtypeStruct((1, runs, 32, 8, 128), F32),
         compiler_params=limit(12),
         cost_estimate=pl.CostEstimate(flops=10**8, bytes_accessed=4 << 20, transcendentals=0),
         name="spectral",
@@ -510,7 +515,7 @@
         name="local",
     )(*orients, kappa_t, phase_field)
 
-    per_step = 2
+    per_step = 8
     whole = pl.BlockSpec((per_step, SLAB, NY, NZ), lambda i: (i, 0, 0, 0))
     phase_next, stress = pl.pallas_call(
         update_kernel,

time: 109 us -> 107 us (0.982)
  Pallas kernels: 19.3 us -> 17.9 us
  starting transfers between devices: 20 us -> 21.3 us
    pallas_call x1, Pallas kernels: 5.89 us -> 4.43 us  [step(): pl.pallas_call(update_kernel, grid=(variants // per_step,), in_specs=[sme...]
where the time goes in v4:
time: 107 us
  blocking collectives  33.8 us (32%)
  waiting for transfers between devices  32.6 us (30%)
  starting transfers between devices  21.3 us (20%)
  Pallas kernels  17.9 us (17%)
    all_to_all x1, blocking collectives, exchange(): lax.all_to_all(value, ('gx', 'vert'), split_axis=0, concat_axis=0, axis_i...  33.8 us
    ppermute x1, waiting for transfers between devices, step(): far = lax.ppermute(far, both, across)  13.1 us
    all_to_all x1, waiting for transfers between devices, exchange(): lax.all_to_all(value, ('gx', 'vert'), split_axis=0, concat_axis=0, axis_i...  11.2 us
    all_to_all x1, starting transfers between devices, exchange(): lax.all_to_all(value, ('gx', 'vert'), split_axis=0, concat_axis=0, axis_i...  7.52 us
    ppermute x1, waiting for transfers between devices, step(): carry = lax.ppermute(relay, both, carried)  6.34 us
    ppermute x1, starting transfers between devices, step(): far = lax.ppermute(far, both, across)  5.71 us
    pallas_call x1, Pallas kernels, step(): pl.pallas_call(update_kernel, grid=(variants // per_step,), in_specs=[sme...  4.43 us
    pallas_call x1, Pallas kernels, step(): pl.pallas_call(local_kernel, in_specs=[smem()] * 3 + [vmem()], out_specs=...  4.21 us
  transfers between devices with their start and end apart: 8, of which 4 were waited for; matrix products, arithmetic and copies ran while one was open for 0% of the time, Pallas kernels for 6%

profile of v4, /device:TPU:32, one launch (start us, length us, event | category | flops | bytes accessed | tf_op | source)
XLA Modules:
  0.0 106.7 jit_solution(7767526047581233051)
XLA Ops:
  0.7 0.1 pad_add_fusion.place_ref
  0.8 0.0 copy-start.1
  0.8 4.2 %sums.1 = (f32[1024,128]{1,0:T(8,128)S(1)}, f32[1024,128]{1,0:T(8,128)S(1)}, f32[16,32,256]{2,1,0:T(8,128)}, f32[16,32,256]{2,1,0:T(8,128)}, f32[8,32,256]{2,1,0:T(8,128)}, /*index=5*/f32[8,32,256]{2,1,0:T(8,128)}) custom-call(s32[3]{0:T(128)S(1)} %pad_add_fusion.place_ref, s32[16]{0:T(128)} %family_ref.1, f32[6,12]{1,0:T(8,128)} %bitcast.13, ...), custom_call_target="tpu_custom_call" | custom-call | flops 100000000 | bytes 9437184 | tf_op jit(solution)/shard_map/sums/pallas_call | solution.py:445
  4.9 0.1 collective-permute-start
  5.0 1.9 %collective-permute-done = f32[1024,128]{1,0:T(8,128)S(1)} collective-permute-done((f32[1024,128]{1,0:T(8,128)S(1)}, f32[1024,128]{1,0:T(8,128)S(1)}, u32[]{:S(2)}, u32[]{:S(2)}) %collective-permute-start) | collective-permute-done | bytes 524320 | tf_op jit(solution)/shard_map/ppermute | solution.py:472
  6.9 0.1 add_bitcast_fusion
  7.0 0.0 copy-start.7
  7.0 0.0 copy-start.5
  7.0 0.0 copy-start
  7.1 0.0 copy-start.4
  7.1 33.8 %all_to_all.10 = f32[128,8,128]{2,1,0:T(8,128)S(1)} all-to-all(f32[128,8,128]{2,1,0:T(8,128)S(1)} %add_bitcast_fusion), channel_id=1, replica_groups={{0,64,128,192,8,72,136,200,16,80,144,208,24,88,152,216,32,96,160,224,40..., dimensions={0} | all-to-all | bytes 1048576 | tf_op jit(solution)/shard_map/all_to_all | solution.py:468
  40.8 0.0 copy-done.1
  40.8 3.0 %spectral.1 = f32[1,4,32,8,128]{4,3,2,1,0:T(8,128)} custom-call(s32[3]{0:T(128)S(1)} %pad_add_fusion.place_ref, f32[1,4,32,8,128]{4,3,2,1,0:T(8,128)S(1)} %bitcast.12, bf16[896,512]{1,0:T(8,128)(2,1)S(1)} %copy-done.1), custom_call_target="tpu_custom_call" | custom-call | flops 100000000 | bytes 4194304 | tf_op jit(solution)/shard_map/spectral/pallas_call | solution.py:484
  43.8 7.5 %all-to-all-start.1 = ((f32[128,8,128]{2,1,0:T(8,128)}), f32[128,8,128]{2,1,0:T(8,128)S(1)}, u32[]{:S(2)}, u32[]{:S(2)}) async-start(f32[128,8,128]{2,1,0:T(8,128)} %bitcast.6), calls=%async_computation.1 | async-start | bytes 1048576 | tf_op jit(solution)/shard_map/all_to_all | solution.py:468
  51.3 4.1 %collective-permute-start.5 = (f32[8,32,256]{2,1,0:T(8,128)}, f32[8,32,256]{2,1,0:T(8,128)}, u32[]{:S(2)}, u32[]{:S(2)}) collective-permute-start(f32[8,32,256]{2,1,0:T(8,128)} %get-tuple-element.15), channel_id=1, source_target_pairs={{24,16},{0,8},{25,17},{1,9},{26,18},{2,10},{27,19},{3,11},{28,20},... | collective-permute-start | bytes 786440 | tf_op jit(solution)/shard_map/ppermute | solution.py:476
  55.5 1.3 %collective-permute-start.2 = (f32[16,32,256]{2,1,0:T(8,128)}, f32[16,32,256]{2,1,0:T(8,128)S(1)}, u32[]{:S(2)}, u32[]{:S(2)}) collective-permute-start(f32[16,32,256]{2,1,0:T(8,128)} %get-tuple-element.12), channel_id=1, source_target_pairs={{0,8},{8,16},{16,24},{1,9},{9,17},{17,25},{2,10},{10,18},{18,26},{... | collective-permute-start | bytes 1572872 | tf_op jit(solution)/shard_map/ppermute | solution.py:477
  56.8 1.3 %collective-permute-start.3 = (f32[16,32,256]{2,1,0:T(8,128)}, f32[16,32,256]{2,1,0:T(8,128)}, u32[]{:S(2)}, u32[]{:S(2)}) collective-permute-start(f32[16,32,256]{2,1,0:T(8,128)} %get-tuple-element.13), channel_id=1, source_target_pairs={{8,0},{16,8},{24,16},{9,1},{17,9},{25,17},{10,2},{18,10},{26,18},{... | collective-permute-start | bytes 1572872 | tf_op jit(solution)/shard_map/ppermute | solution.py:478
  58.1 11.2 %all-to-all-done.1 = f32[128,8,128]{2,1,0:T(8,128)S(1)} async-done(((f32[128,8,128]{2,1,0:T(8,128)}), f32[128,8,128]{2,1,0:T(8,128)S(1)}, u32[]{:S(2)}, u32[]{:S(2)}) %all-to-all-start.1) | async-done | bytes 524320 | tf_op jit(solution)/shard_map/all_to_all | solution.py:468
  69.3 0.0 collective-permute-start.1
  69.3 0.0 copy-done.7
  69.3 5.7 %collective-permute-start.4 = (f32[8,32,256]{2,1,0:T(8,128)S(1)}, f32[8,32,256]{2,1,0:T(8,128)S(1)}, u32[]{:S(2)}, u32[]{:S(2)}) collective-permute-start(f32[8,32,256]{2,1,0:T(8,128)S(1)} %copy-done.7), channel_id=1, source_target_pairs={{24,32},{0,248},{25,33},{1,249},{26,34},{2,250},{27,35},{3,251},{2... | collective-permute-start | bytes 786440 | tf_op jit(solution)/shard_map/ppermute | solution.py:479
  75.0 0.0 collective-permute-done.5
  75.0 1.3 %collective-permute-start.6 = (f32[8,32,256]{2,1,0:T(8,128)}, f32[8,32,256]{2,1,0:T(8,128)S(1)}, u32[]{:S(2)}, u32[]{:S(2)}) collective-permute-start(f32[8,32,256]{2,1,0:T(8,128)} %collective-permute-done.5), channel_id=1, source_target_pairs={{16,32},{8,248},{17,33},{9,249},{18,34},{10,250},{19,35},{11,251},... | collective-permute-start | bytes 786440 | tf_op jit(solution)/shard_map/ppermute | solution.py:480
  76.3 0.0 copy-done.5
  76.3 0.1 fusion
  76.4 0.0 copy-done
  76.4 0.0 copy-done.4
  76.4 0.0 copy-start.2
  76.4 0.0 copy-start.3
  76.4 0.0 copy-start.6
  76.4 4.2 %local.1.part_hbm = f32[16,4,32,256]{3,2,1,0:T(8,128)} custom-call(s32[8]{0:T(128)S(1)} %get-tuple-element.19.orient_low, s32[8]{0:T(128)S(1)} %get-tuple-element.18.orient_high, f32[3,24]{1,0:T(4,128)S(1)} %bitcast.15, f32[16,4,32,256]{3,2,1,0:T(8,128)S(1)} %copy-done), custom_call_target="tpu_custom_call" | custom-call | flops 10000000 | bytes 10485760 | tf_op jit(solution)/shard_map/local/pallas_call | solution.py:508
  80.6 13.1 %collective-permute-done.4.far = f32[8,32,256]{2,1,0:T(8,128)S(1)} collective-permute-done((f32[8,32,256]{2,1,0:T(8,128)S(1)}, f32[8,32,256]{2,1,0:T(8,128)S(1)}, u32[]{:S(2)}, u32[]{:S(2)}) %collective-permute-start.4) | collective-permute-done | bytes 262176 | tf_op jit(solution)/shard_map/ppermute | solution.py:479
  93.8 6.3 %collective-permute-done.6.carried = f32[8,32,256]{2,1,0:T(8,128)S(1)} collective-permute-done((f32[8,32,256]{2,1,0:T(8,128)}, f32[8,32,256]{2,1,0:T(8,128)S(1)}, u32[]{:S(2)}, u32[]{:S(2)}) %collective-permute-start.6) | collective-permute-done | bytes 262176 | tf_op jit(solution)/shard_map/ppermute | solution.py:480
  100.1 0.0 collective-permute-done.2.near_low
  100.1 0.0 collective-permute-done.3.near_high
  100.1 2.1 %edges.1 = (f32[16,32,256]{2,1,0:T(8,128)}, f32[16,32,256]{2,1,0:T(8,128)}) custom-call(s32[3]{0:T(128)S(1)} %pad_add_fusion.place_ref, s32[16]{0:T(128)S(1)} %copy-done.5, f32[3,24]{1,0:T(4,128)S(1)} %bitcast.16, f32[16,32,256]{2,1,0:T(8,128)S(1)} %collective-permute-done.2.near_low, f32[16,32,256]{2,1,0:T(8,128)} %collective-permute-done.3.near_high, ...), custom_call_target="tpu_custom_call" | custom-call | flops 1000000 | bytes 3145728 | tf_op jit(solution)/shard_map/edges/pallas_call | solution.py:497
  102.2 0.0 collective-permute-done.1.other_ref
  102.2 0.0 copy-done.2
  102.2 0.0 copy-done.3
  102.2 0.0 copy-done.6
  102.3 4.4 %update.1 = (f32[16,4,32,256]{3,2,1,0:T(8,128)}, f32[6,4,32,256]{3,2,1,0:T(8,128)}) custom-call(s32[3]{0:T(128)S(1)} %pad_add_fusion.place_ref, s32[16]{0:T(128)S(1)} %copy-done.6, f32[6,12]{1,0:T(8,128)S(1)} %bitcast.14, f32[1024,128]{1,0:T(8,128)S(1)} %bitcast.11, f32[1024,128]{1,0:T(8,128)S(1)} %collective-permute-done.1.other_ref, ...), custom_call_target="tpu_custom_call" | custom-call | flops 100000000 | bytes 12582912 | tf_op jit(solution)/shard_map/update/pallas_call | solution.py:520
Async XLA Ops:
  0.8 40.1 %copy-start.1 = (bf16[896,512]{1,0:T(8,128)(2,1)S(1)}, bf16[896,512]{1,0:T(8,128)(2,1)}, u32[]{:S(2)}) copy-start(bf16[896,512]{1,0:T(8,128)(2,1)} %constant.78.clone.table) | copy-start | bytes 2752516
  4.9 2.0 %collective-permute-start = (f32[1024,128]{1,0:T(8,128)S(1)}, f32[1024,128]{1,0:T(8,128)S(1)}, u32[]{:S(2)}, u32[]{:S(2)}) collective-permute-start(f32[1024,128]{1,0:T(8,128)S(1)} %get-tuple-element.11), channel_id=1, source_target_pairs={{0,1},{1,0},{2,3},{3,2},{4,5},{5,4},{6,7},{7,6},{8,9},{9,8},{10,11... | collective-permute-start | bytes 1572872 | tf_op jit(solution)/shard_map/ppermute | solution.py:472
  7.0 62.3 %copy-start.7 = (f32[8,32,256]{2,1,0:T(8,128)S(1)}, f32[8,32,256]{2,1,0:T(8,128)}, u32[]{:S(2)}) copy-start(f32[8,32,256]{2,1,0:T(8,128)} %get-tuple-element.14) | copy-start | bytes 786436
  7.0 69.3 %copy-start.5 = (s32[16]{0:T(128)S(1)}, s32[16]{0:T(128)}, u32[]{:S(2)}) copy-start(s32[16]{0:T(128)} %orient_ref.1) | copy-start | bytes 196
  7.0 69.4 %copy-start = (f32[16,4,32,256]{3,2,1,0:T(8,128)S(1)}, f32[16,4,32,256]{3,2,1,0:T(8,128)}, u32[]{:S(2)}) copy-start(f32[16,4,32,256]{3,2,1,0:T(8,128)} %phase_ref.3) | copy-start | bytes 6291460
  7.1 69.4 %copy-start.4 = (f32[24,3]{0,1:T(4,128)S(1)}, f32[24,3]{0,1:T(4,128)}, u32[]{:S(2)}) copy-start(f32[24,3]{0,1:T(4,128)} %param.9) | copy-start | bytes 868
  43.8 25.5 %all-to-all-start.1 = ((f32[128,8,128]{2,1,0:T(8,128)}), f32[128,8,128]{2,1,0:T(8,128)S(1)}, u32[]{:S(2)}, u32[]{:S(2)}) async-start(f32[128,8,128]{2,1,0:T(8,128)} %bitcast.6), calls=%async_computation.1 | async-start | bytes 1048576 | tf_op jit(solution)/shard_map/all_to_all | solution.py:468
  51.3 23.7 %collective-permute-start.5 = (f32[8,32,256]{2,1,0:T(8,128)}, f32[8,32,256]{2,1,0:T(8,128)}, u32[]{:S(2)}, u32[]{:S(2)}) collective-permute-start(f32[8,32,256]{2,1,0:T(8,128)} %get-tuple-element.15), channel_id=1, source_target_pairs={{24,16},{0,8},{25,17},{1,9},{26,18},{2,10},{27,19},{3,11},{28,20},... | collective-permute-start | bytes 786440 | tf_op jit(solution)/shard_map/ppermute | solution.py:476
  55.5 44.7 %collective-permute-start.2 = (f32[16,32,256]{2,1,0:T(8,128)}, f32[16,32,256]{2,1,0:T(8,128)S(1)}, u32[]{:S(2)}, u32[]{:S(2)}) collective-permute-start(f32[16,32,256]{2,1,0:T(8,128)} %get-tuple-element.12), channel_id=1, source_target_pairs={{0,8},{8,16},{16,24},{1,9},{9,17},{17,25},{2,10},{10,18},{18,26},{... | collective-permute-start | bytes 1572872 | tf_op jit(solution)/shard_map/ppermute | solution.py:477
  56.8 43.3 %collective-permute-start.3 = (f32[16,32,256]{2,1,0:T(8,128)}, f32[16,32,256]{2,1,0:T(8,128)}, u32[]{:S(2)}, u32[]{:S(2)}) collective-permute-start(f32[16,32,256]{2,1,0:T(8,128)} %get-tuple-element.13), channel_id=1, source_target_pairs={{8,0},{16,8},{24,16},{9,1},{17,9},{25,17},{10,2},{18,10},{26,18},{... | collective-permute-start | bytes 1572872 | tf_op jit(solution)/shard_map/ppermute | solution.py:478
  69.3 32.9 %collective-permute-start.1 = (f32[1024,128]{1,0:T(8,128)S(1)}, f32[1024,128]{1,0:T(8,128)S(1)}, u32[]{:S(2)}, u32[]{:S(2)}) collective-permute-start(f32[1024,128]{1,0:T(8,128)S(1)} %bitcast.10), channel_id=1, source_target_pairs={{0,1},{1,0},{2,3},{3,2},{4,5},{5,4},{6,7},{7,6},{8,9},{9,8},{10,11... | collective-permute-start | bytes 1572872 | tf_op jit(solution)/shard_map/ppermute | solution.py:495
  69.3 24.5 %collective-permute-start.4 = (f32[8,32,256]{2,1,0:T(8,128)S(1)}, f32[8,32,256]{2,1,0:T(8,128)S(1)}, u32[]{:S(2)}, u32[]{:S(2)}) collective-permute-start(f32[8,32,256]{2,1,0:T(8,128)S(1)} %copy-done.7), channel_id=1, source_target_pairs={{24,32},{0,248},{25,33},{1,249},{26,34},{2,250},{27,35},{3,251},{2... | collective-permute-start | bytes 786440 | tf_op jit(solution)/shard_map/ppermute | solution.py:479
  75.0 25.1 %collective-permute-start.6 = (f32[8,32,256]{2,1,0:T(8,128)}, f32[8,32,256]{2,1,0:T(8,128)S(1)}, u32[]{:S(2)}, u32[]{:S(2)}) collective-permute-start(f32[8,32,256]{2,1,0:T(8,128)} %collective-permute-done.5), channel_id=1, source_target_pairs={{16,32},{8,248},{17,33},{9,249},{18,34},{10,250},{19,35},{11,251},... | collective-permute-start | bytes 786440 | tf_op jit(solution)/shard_map/ppermute | solution.py:480
  76.4 25.8 %copy-start.2 = (bf16[6,256,256]{2,1,0:T(8,128)(2,1)S(1)}, bf16[6,256,256]{2,1,0:T(8,128)(2,1)}, u32[]{:S(2)}) copy-start(bf16[6,256,256]{2,1,0:T(8,128)(2,1)} %constant.79.clone.table) | copy-start | bytes 2359300
  76.4 25.8 %copy-start.3 = (f32[12,6]{0,1:T(8,128)S(1)}, f32[12,6]{0,1:T(8,128)}, u32[]{:S(2)}) copy-start(f32[12,6]{0,1:T(8,128)} %param.10) | copy-start | bytes 868
  76.4 25.8 %copy-start.6 = (s32[16]{0:T(128)S(1)}, s32[16]{0:T(128)}, u32[]{:S(2)}) copy-start(s32[16]{0:T(128)} %family_ref.1) | copy-start | bytes 196
